TPU v7x, 128 devices: a whole 4x4x4 slice. The times are simulated.
128 devices in a mesh: mesh: 32 (over z_lo, x, y), harm: 4 (over z_hi, core).
Axes of the slice: x: 4, y: 4, z: 4 (z_hi: 2, z_lo: 2; z = z_hi * 2 + z_lo), core: 2. Of those that a mesh axis runs over, the one named last changes fastest.
Arguments:
- field_in: float32 [64, 163840], P('harm', 'mesh'), may hold values from -6 to 6
- faces: int32 [2, 32768], P(None, 'mesh'), may hold values from 0 to 5119, as said below
- connectivity: int32 [6, 131072], P(None, 'mesh'), may hold values from 0 to 7167
- curl_vectors: float32 [3, 6, 131072], P(None, None, 'mesh'), may hold values from -2.4 to 2.4
- operating_point: float32 [64, 3, 32, 4096], P(None, None, None, ('mesh', 'harm')), may hold values from -2.5 to 2.5
- material: int32 [32, 4096], P(None, ('mesh', 'harm')), may hold values from 0 to 3
- bh_knots: int32 [8], replicated, may hold values from 0 to 15
- curve_base: float32 [4], replicated, may hold values from 0.5 to 2
- curve_slopes: float32 [4, 8], replicated, may hold values from 0.02 to 0.2
Outputs:
- product: float32 [64, 163840], P('harm', 'mesh')
Inputs may be any that keep to these rules, and one draw needn't show every extreme that they name: `faces`: for each partition the 1024 lower face edges and the 1024 upper face edges are 2048 distinct local edge numbers. `connectivity`: numbers below 5120 are the partition's own edges, the next 1024 the ghost edges after the upper face list of the partition below, the last 1024 those after the lower face list of the partition above.
All inputs are finite; a program needn't handle non-finite values.
Results may differ from a plain program's by a relative error of at most 0.0003.
Values sent between devices are 32-bit elements; how exact they have to be, the bound alone decides.
A program may use at most 128 MiB of HBM per device.

v0:
```python
import functools

import numpy as np
import jax
import jax.numpy as jnp
from jax import lax
from jax.experimental import pallas as pl
from jax.experimental.pallas import tpu as pltpu
from jax.sharding import PartitionSpec as P

MESH = pl.DeviceIdType.MESH
N_MESH = 32
OWN = 5120
FACE = 1024
EXT = OWN + 2 * FACE
ROWS = 512
MSG = 56


def block_diag_tables():
    length = 64
    t = np.arange(length)
    c = np.arange(length)
    freq = np.where(c < 32, c, c - 31)
    freq[-1] = 32
    sine = (c >= 32) & (c < 63)
    angle = 2.0 * np.pi * ((freq[:, None] * t[None, :]) % length) / length
    basis = np.where(sine[:, None], np.sin(angle), np.cos(angle))
    weight = np.where((c == 0) | (c == 63), 1.0 / length, 2.0 / length)
    inverse = np.kron(np.eye(2), basis)
    forward = np.kron(np.eye(2), (basis * weight[:, None]).T)
    return inverse.astype(np.float32), forward.astype(np.float32)


def spread_kernel(field_ref, faces_ref, point_ref, mat_ref, ext_out, op_out,
                  opsend, field_t, face_rows, face_cols,
                  op_ss, op_rs, own_ss, own_rs, gh_ss, gh_rs, fw_ss, fw_rs, lo_s):
    m = lax.axis_index("mesh")
    h = lax.axis_index("harm")
    up, down = lax.rem(m + 1, N_MESH), lax.rem(m + N_MESH - 1, N_MESH)
    side = h + 1 - 2 * lax.rem(h, 2)
    far = lax.rem(h + 2, 4)

    barrier = pltpu.get_barrier_semaphore()

    @pl.loop(1, N_MESH)
    def _(d):
        pl.semaphore_signal(barrier, inc=1, device_id=(lax.rem(m + d, N_MESH), h), device_id_type=MESH)
    for peer in (side, far):
        pl.semaphore_signal(barrier, inc=1, device_id=(m, peer), device_id_type=MESH)

    lane = lax.broadcasted_iota(jnp.int32, (16, 64), 1)
    del lane

    @pl.loop(0, N_MESH)
    def _(p):
        for i in range(3):
            opsend[p, pl.ds(16 * i, 16), pl.ds(0, 64)] = point_ref[i, p, pl.ds(0, 16), :]
            opsend[p, pl.ds(16 * i, 16), pl.ds(64, 64)] = point_ref[i, p, pl.ds(16, 16), :]
        opsend[p, pl.ds(48, 8), :] = jnp.zeros((8, 128), jnp.float32)
        opsend[p, pl.ds(48, 1), pl.ds(0, 32)] = mat_ref[pl.ds(p, 1), :].astype(jnp.float32)

    pl.semaphore_wait(barrier, N_MESH - 1 + 2)

    rows = pl.ds(pl.multiple_of(16 * h, 16), 16)
    own_cols = pl.ds(0, OWN)
    ghost_cols = pl.ds(OWN, 2 * FACE)

    def own_copy(n, peer):
        return pltpu.make_async_remote_copy(
            src_ref=field_ref, dst_ref=ext_out.at[rows, own_cols],
            send_sem=own_ss.at[n], recv_sem=own_rs.at[n],
            device_id=(m, peer), device_id_type=MESH)

    own_far, own_side = own_copy(0, far), own_copy(1, side)
    own_far.start()
    own_side.start()
    local = pltpu.make_async_copy(field_ref, ext_out.at[rows, own_cols], lo_s)
    local.start()

    def op_copy(d):
        p = lax.rem(m + d, N_MESH)
        return pltpu.make_async_remote_copy(
            src_ref=opsend.at[p], dst_ref=op_out.at[m],
            send_sem=op_ss.at[d], recv_sem=op_rs.at[d],
            device_id=(p, h), device_id_type=MESH)

    @pl.loop(1, N_MESH)
    def _(d):
        op_copy(d).start()
    op_local = pltpu.make_async_copy(opsend.at[m], op_out.at[m], op_ss.at[0])
    op_local.start()

    @pl.loop(0, OWN // 128, unroll=4)
    def _(b):
        at = pl.ds(pl.multiple_of(b * 128, 128), 128)
        field_t[at, :] = field_ref[:, at].T

    for f in range(2):
        @pl.loop(0, FACE // 16)
        def _(b):
            for k in range(16):
                n = faces_ref[f, b * 16 + k]
                face_rows[pl.ds(f * FACE + b * 16 + k, 1), :] = field_t[pl.ds(n, 1), :]

    @pl.loop(0, 2 * FACE // 128, unroll=4)
    def _(b):
        at = pl.ds(pl.multiple_of(b * 128, 128), 128)
        face_cols[:, at] = face_rows[at, :].T

    def ghost_copy(f, peer):
        return pltpu.make_async_remote_copy(
            src_ref=face_cols.at[:, pl.ds(f * FACE, FACE)],
            dst_ref=ext_out.at[rows, pl.ds(OWN + (1 - f) * FACE, FACE)],
            send_sem=gh_ss.at[f], recv_sem=gh_rs.at[f],
            device_id=(peer, h), device_id_type=MESH)

    ghosts = [ghost_copy(0, down), ghost_copy(1, up)]
    for c in ghosts:
        c.start()
    for c in ghosts:
        c.wait_recv()

    def gfwd_copy(n, peer):
        return pltpu.make_async_remote_copy(
            src_ref=ext_out.at[rows, ghost_cols], dst_ref=ext_out.at[rows, ghost_cols],
            send_sem=fw_ss.at[n], recv_sem=fw_rs.at[n],
            device_id=(m, peer), device_id_type=MESH)

    gfar, gside = gfwd_copy(0, far), gfwd_copy(1, side)
    gfar.start()
    gside.start()

    far_rows = pl.ds(pl.multiple_of(16 * far, 16), 16)

    def relay(n, cols):
        return pltpu.make_async_remote_copy(
            src_ref=ext_out.at[far_rows, cols], dst_ref=ext_out.at[far_rows, cols],
            send_sem=fw_ss.at[n], recv_sem=fw_rs.at[n],
            device_id=(m, side), device_id_type=MESH)

    own_far.wait_recv()
    relay_own = relay(2, own_cols)
    relay_own.start()
    gfar.wait_recv()
    relay_gh = relay(3, ghost_cols)
    relay_gh.start()

    own_side.wait_recv()
    gside.wait_recv()
    relay_own.wait_recv()
    relay_gh.wait_recv()

    @pl.loop(1, N_MESH)
    def _(d):
        op_copy(d).wait_recv()

    local.wait()
    op_local.wait()
    for c in (own_far, own_side, gfar, gside, relay_own, relay_gh, *ghosts):
        c.wait_send()

    @pl.loop(1, N_MESH)
    def _(d):
        op_copy(d).wait_send()


def spread(field_in, faces, point, material):
    return pl.pallas_call(
        spread_kernel,
        name="spread",
        out_shape=(jax.ShapeDtypeStruct((64, EXT), jnp.float32),
                   jax.ShapeDtypeStruct((N_MESH, MSG, 128), jnp.float32)),
        in_specs=[pl.BlockSpec(memory_space=pltpu.VMEM), pl.BlockSpec(memory_space=pltpu.SMEM),
                  pl.BlockSpec(memory_space=pltpu.VMEM), pl.BlockSpec(memory_space=pltpu.VMEM)],
        out_specs=(pl.BlockSpec(memory_space=pl.ANY), pl.BlockSpec(memory_space=pl.ANY)),
        scratch_shapes=[
            pltpu.VMEM((N_MESH, MSG, 128), jnp.float32),
            pltpu.VMEM((OWN, 16), jnp.float32),
            pltpu.VMEM((2 * FACE, 16), jnp.float32),
            pltpu.VMEM((16, 2 * FACE), jnp.float32),
            pltpu.SemaphoreType.DMA((N_MESH,)), pltpu.SemaphoreType.DMA((N_MESH,)),
            pltpu.SemaphoreType.DMA((2,)), pltpu.SemaphoreType.DMA((2,)),
            pltpu.SemaphoreType.DMA((2,)), pltpu.SemaphoreType.DMA((2,)),
            pltpu.SemaphoreType.DMA((4,)), pltpu.SemaphoreType.DMA((4,)),
            pltpu.SemaphoreType.DMA,
        ],
        compiler_params=pltpu.CompilerParams(collective_id=0, has_side_effects=True,
                                             vmem_limit_bytes=40 << 20),
    )(field_in, faces, point, material)


def element_kernel(conn_ref, knots_ref, base_ref, slopes_ref, ext_ref, op_ref, curl_ref, inv_ref, fwd_ref,
                   out_ref, ext2, curl_t, mat_b, wide, got, flux, acc0, acc1, acc2, acc3):
    h = lax.axis_index("harm")
    low = lax.broadcasted_iota(jnp.int32, (16, 128), 1) < 64
    low1 = lax.broadcasted_iota(jnp.int32, (1, 128), 1) < 64
    accs = (acc0, acc1, acc2, acc3)

    @pl.loop(0, EXT // 128, unroll=2)
    def _(b):
        at = pl.ds(pl.multiple_of(b * 128, 128), 128)
        x = ext_ref[:, at]
        ext2[at, :] = jnp.concatenate([x, x], axis=0).T

    @pl.loop(0, EXT // 64)
    def _(b):
        at = pl.ds(pl.multiple_of(b * 64, 64), 64)
        for a in accs:
            a[at, :] = jnp.zeros((64, 128), jnp.float32)

    @pl.loop(0, N_MESH)
    def _(m):
        at = pl.ds(pl.multiple_of(m * 128, 128), 128)
        pad = jnp.zeros((2, 128), jnp.float32)
        parts = []
        for i in range(3):
            parts += [curl_ref[i, :, at], pad]
        curl_t[at, :] = jnp.concatenate(parts, axis=0).T

    @pl.loop(0, N_MESH)
    def _(m):
        to = pl.ds(pl.multiple_of(m * 16, 16), 16)
        first = m * 128 + h * 32
        c0 = curl_t[pl.ds(pl.multiple_of(first, 16), 16), :]
        c1 = curl_t[pl.ds(pl.multiple_of(first + 16, 16), 16), :]
        for i in range(3):
            for j in range(6):
                col = i * 8 + j
                wide[i * 6 + j, to, :] = jnp.where(low, jnp.broadcast_to(c0[:, col:col + 1], (16, 128)),
                                                   jnp.broadcast_to(c1[:, col:col + 1], (16, 128)))
        mt = jnp.broadcast_to(op_ref[m, pl.ds(48, 1), :], (8, 128)).T
        mat_b[to, :] = jnp.where(low, jnp.broadcast_to(mt[0:16, 0:1], (16, 128)),
                                 jnp.broadcast_to(mt[16:32, 0:1], (16, 128)))

    @pl.loop(0, N_MESH)
    def _(m):
        to = pl.ds(pl.multiple_of(m * 16, 16), 16)
        first = m * 128 + h * 32
        for j in range(6):
            for k in range(16):
                a = ext2[pl.ds(conn_ref[j, first + k], 1), :]
                b = ext2[pl.ds(conn_ref[j, first + 16 + k], 1), :]
                got[pl.ds(j * 16 + k, 1), :] = jnp.where(low1, a, b)
        for i in range(3):
            s = wide[i * 6, to, :] * got[0:16, :]
            for j in range(1, 6):
                s = s + wide[i * 6 + j, to, :] * got[j * 16:(j + 1) * 16, :]
            flux[i, to, :] = s

    growth = [jnp.exp(jnp.float32(-0.5) * knots_ref[k].astype(jnp.float32)) for k in range(8)]

    @pl.loop(0, ROWS // 64)
    def _(r):
        to = pl.ds(pl.multiple_of(r * 64, 64), 64)
        f = [jnp.dot(flux[i, to, :], inv_ref[...], precision=lax.Precision.HIGHEST,
                     preferred_element_type=jnp.float32) for i in range(3)]
        b = [jnp.concatenate([op_ref[r * 4 + s, 16 * i:16 * i + 16, :] for s in range(4)], axis=0)
             for i in range(3)]
        mat = mat_b[to, :]

        def pick(values):
            x = jnp.where(mat == 1.0, values[1], values[0])
            x = jnp.where(mat == 2.0, values[2], x)
            return jnp.where(mat == 3.0, values[3], x)

        q = b[0] * b[0] + b[1] * b[1] + b[2] * b[2]
        u = jnp.exp(2.0 * q)
        nu = pick([base_ref[a] for a in range(4)])
        dnu = jnp.zeros_like(q)
        for k in range(8):
            slope = pick([slopes_ref[a, k] for a in range(4)])
            e = u * growth[k]
            w = 1.0 + e
            nu = nu + slope * jnp.log(w)
            dnu = dnu + slope * (e / w)
        proj = b[0] * f[0] + b[1] * f[1] + b[2] * f[2]
        scale = 4.0 * dnu * proj
        for i in range(3):
            flux[i, to, :] = jnp.dot(nu * f[i] + scale * b[i], fwd_ref[...], precision=lax.Precision.HIGHEST,
                                     preferred_element_type=jnp.float32)

    @pl.loop(0, N_MESH)
    def _(m):
        to = pl.ds(pl.multiple_of(m * 16, 16), 16)
        first = m * 128 + h * 32
        f = [flux[i, to, :] for i in range(3)]
        for j in range(6):
            got[j * 16:(j + 1) * 16, :] = (wide[j, to, :] * f[0] + wide[6 + j, to, :] * f[1]
                                           + wide[12 + j, to, :] * f[2])
        for k in range(16):
            for j in range(0, 6, 2):
                for jj in range(2):
                    row = got[pl.ds((j + jj) * 16 + k, 1), :]
                    n0 = conn_ref[j + jj, first + k]
                    n1 = conn_ref[j + jj, first + 16 + k]
                    accs[jj][pl.ds(n0, 1), :] = accs[jj][pl.ds(n0, 1), :] + row
                    accs[2 + jj][pl.ds(n1, 1), :] = accs[2 + jj][pl.ds(n1, 1), :] + row

    wide_low = lax.broadcasted_iota(jnp.int32, (128, 128), 1) < 64

    @pl.loop(0, EXT // 128)
    def _(b):
        at = pl.ds(pl.multiple_of(b * 128, 128), 128)
        x = jnp.where(wide_low, acc0[at, :] + acc1[at, :], acc2[at, :] + acc3[at, :]).T
        out_ref[:, at] = x[0:64, :] + x[64:128, :]


def elements(conn, knots, base, slopes, ext, op, curl):
    inverse, forward = block_diag_tables()
    smem = pl.BlockSpec(memory_space=pltpu.SMEM)
    vmem = pl.BlockSpec(memory_space=pltpu.VMEM)
    big = pltpu.VMEM((EXT, 128), jnp.float32)
    return pl.pallas_call(
        element_kernel,
        name="elements",
        out_shape=jax.ShapeDtypeStruct((64, EXT), jnp.float32),
        in_specs=[smem, smem, smem, smem, vmem, vmem, vmem, vmem, vmem],
        out_specs=vmem,
        scratch_shapes=[big, pltpu.VMEM((4096, 24), jnp.float32), pltpu.VMEM((ROWS, 128), jnp.float32),
                        pltpu.VMEM((18, ROWS, 128), jnp.float32), pltpu.VMEM((96, 128), jnp.float32),
                        pltpu.VMEM((3, ROWS, 128), jnp.float32), big, big, big, big],
        compiler_params=pltpu.CompilerParams(vmem_limit_bytes=60 << 20),
    )(conn, knots, base, slopes, ext, op, curl, jnp.asarray(inverse), jnp.asarray(forward))


def combine_kernel(acc_ref, own_out, ghost_out, pairs, summed, zin, ghost_sum,
                   p_ss, p_rs, z_ss, z_rs, g_ss, g_rs):
    m = lax.axis_index("mesh")
    h = lax.axis_index("harm")
    up, down = lax.rem(m + 1, N_MESH), lax.rem(m + N_MESH - 1, N_MESH)
    side = h + 1 - 2 * lax.rem(h, 2)
    far = lax.rem(h + 2, 4)
    cross = lax.rem(side + 2, 4)
    barrier = pltpu.get_barrier_semaphore()
    peers = ((m, side), (m, far), (up, h), (down, h))
    for peer in peers:
        pl.semaphore_signal(barrier, inc=1, device_id=peer, device_id_type=MESH)
    pl.semaphore_wait(barrier, 4)

    chunks = (pl.ds(OWN, 2 * FACE), pl.ds(0, OWN))

    def block(who):
        return pl.ds(pl.multiple_of(16 * who, 16), 16)

    def pair_copy(c, n):
        who = (side, cross)[n]
        return pltpu.make_async_remote_copy(
            src_ref=acc_ref.at[block(who), chunks[c]], dst_ref=pairs.at[n, :, chunks[c]],
            send_sem=p_ss.at[c, n], recv_sem=p_rs.at[c, n],
            device_id=(m, side), device_id_type=MESH)

    def z_copy(c):
        return pltpu.make_async_remote_copy(
            src_ref=summed.at[:, chunks[c]], dst_ref=zin.at[:, chunks[c]],
            send_sem=z_ss.at[c], recv_sem=z_rs.at[c],
            device_id=(m, far), device_id_type=MESH)

    def g_copy(f, peer):
        return pltpu.make_async_remote_copy(
            src_ref=ghost_sum.at[:, pl.ds(f * FACE, FACE)],
            dst_ref=ghost_out.at[:, pl.ds((1 - f) * FACE, FACE)],
            send_sem=g_ss.at[f], recv_sem=g_rs.at[f],
            device_id=(peer, h), device_id_type=MESH)

    order = [(0, 1), (1, 1), (0, 0), (1, 0)]
    pair = {cn: pair_copy(*cn) for cn in order}
    for cn in order:
        pair[cn].start()
    zs = [z_copy(0), z_copy(1)]
    for c in range(2):
        pair[c, 1].wait_recv()
        summed[:, chunks[c]] = acc_ref[block(far), chunks[c]] + pairs[1, :, chunks[c]]
        zs[c].start()
    pair[0, 0].wait_recv()
    zs[0].wait_recv()
    ghost_sum[...] = acc_ref[block(h), chunks[0]] + pairs[0, :, chunks[0]] + zin[:, chunks[0]]
    gs = [g_copy(0, down), g_copy(1, up)]
    for g in gs:
        g.start()
    pair[1, 0].wait_recv()
    zs[1].wait_recv()
    own_out[...] = acc_ref[block(h), chunks[1]] + pairs[0, :, chunks[1]] + zin[:, chunks[1]]
    for g in gs:
        g.wait_recv()
    for c in (*pair.values(), *zs, *gs):
        c.wait_send()


def combine(acc):
    vmem = pl.BlockSpec(memory_space=pltpu.VMEM)
    return pl.pallas_call(
        combine_kernel,
        name="combine",
        out_shape=(jax.ShapeDtypeStruct((16, OWN), jnp.float32),
                   jax.ShapeDtypeStruct((16, 2 * FACE), jnp.float32)),
        in_specs=[vmem],
        out_specs=(vmem, pl.BlockSpec(memory_space=pl.ANY)),
        scratch_shapes=[
            pltpu.VMEM((2, 16, EXT), jnp.float32), pltpu.VMEM((16, EXT), jnp.float32),
            pltpu.VMEM((16, EXT), jnp.float32), pltpu.VMEM((16, 2 * FACE), jnp.float32),
            pltpu.SemaphoreType.DMA((2, 2)), pltpu.SemaphoreType.DMA((2, 2)),
            pltpu.SemaphoreType.DMA((2,)), pltpu.SemaphoreType.DMA((2,)),
            pltpu.SemaphoreType.DMA((2,)), pltpu.SemaphoreType.DMA((2,)),
        ],
        compiler_params=pltpu.CompilerParams(collective_id=1, has_side_effects=True,
                                             vmem_limit_bytes=40 << 20),
    )(acc)


def finish_kernel(faces_ref, own_ref, ghost_ref, out_ref, ghost_t, full_t):
    @pl.loop(0, OWN // 128, unroll=4)
    def _(b):
        full_t[pl.ds(pl.multiple_of(b * 128, 128), 128), :] = jnp.zeros((128, 16), jnp.float32)

    @pl.loop(0, 2 * FACE // 128, unroll=4)
    def _(b):
        at = pl.ds(pl.multiple_of(b * 128, 128), 128)
        ghost_t[at, :] = ghost_ref[:, at].T

    for f in range(2):
        @pl.loop(0, FACE // 16)
        def _(b):
            for k in range(16):
                full_t[pl.ds(faces_ref[f, b * 16 + k], 1), :] = ghost_t[pl.ds(f * FACE + b * 16 + k, 1), :]

    @pl.loop(0, OWN // 128, unroll=4)
    def _(b):
        at = pl.ds(pl.multiple_of(b * 128, 128), 128)
        out_ref[:, at] = own_ref[:, at] + full_t[at, :].T


def finish(faces, own, ghost):
    vmem = pl.BlockSpec(memory_space=pltpu.VMEM)
    return pl.pallas_call(
        finish_kernel,
        name="finish",
        out_shape=jax.ShapeDtypeStruct((16, OWN), jnp.float32),
        in_specs=[pl.BlockSpec(memory_space=pltpu.SMEM), vmem, vmem],
        out_specs=vmem,
        scratch_shapes=[pltpu.VMEM((2 * FACE, 16), jnp.float32), pltpu.VMEM((OWN, 16), jnp.float32)],
        compiler_params=pltpu.CompilerParams(vmem_limit_bytes=40 << 20),
    )(faces, own, ghost)


def per_device(field_in, faces, connectivity, curl_vectors, operating_point, material, bh_knots, curve_base,
               curve_slopes):
    point = jnp.transpose(operating_point, (1, 2, 3, 0))
    ext, op = spread(field_in, faces, point, material)
    acc = elements(connectivity, bh_knots, curve_base, curve_slopes, ext, op, curl_vectors)
    own, ghost = combine(acc)
    return finish(faces, own, ghost)


def solution(mesh):
    return jax.shard_map(
        per_device,
        mesh=mesh,
        in_specs=(P("harm", "mesh"), P(None, "mesh"), P(None, "mesh"), P(None, None, "mesh"),
                  P(None, None, None, ("mesh", "harm")), P(None, ("mesh", "harm")), P(), P(), P()),
        out_specs=P("harm", "mesh"),
        check_vma=False,
    )
```

profile of v0, /device:TPU:1, one launch (start us, length us, event | category | flops | bytes accessed | tf_op | source)
XLA Modules:
  0.0 115.5 jit_solution(14791024972678930984)
XLA Ops:
  0.0 0.0 copy-start.2
  0.0 1.4 %copy-done.2 = f32[64,3,32,32]{0,3,2,1:T(8,128)S(1)} copy-done((f32[64,3,32,32]{0,3,2,1:T(8,128)S(1)}, f32[64,3,32,32]{0,3,2,1:T(8,128)}, u32[]{:S(2)}) %copy-start.2) | copy-done | bytes 786456
  1.4 0.0 copy-start.4
  1.4 1.0 copy-done.4
  2.4 0.0 copy-start.5
  2.4 0.7 copy-done.5
  3.1 0.0 copy-start.7
  3.1 0.7 copy-done.7
  3.8 36.3 %spread.1 = (f32[64,7168]{1,0:T(8,128)S(1)}, f32[32,56,128]{2,1,0:T(8,128)S(1)}) custom-call(f32[16,5120]{1,0:T(8,128)S(1)} %copy-done.4, s32[2,1024]{1,0:T(2,128)S(1)} %copy-done.5, f32[3,32,32,64]{3,2,1,0:T(8,128)S(1)} %bitcast.1, s32[32,32]{1,0:T(8,128)S(1)} %copy-done.7), custom_call_target="tpu_custom_call" | custom-call | tf_op jit(solution)/shard_map/spread/pallas_call | solution.py:169
  40.1 0.0 copy-start.1
  40.1 1.2 %copy-done.1 = f32[64,7168]{1,0:T(8,128)} copy-done((f32[64,7168]{1,0:T(8,128)}, f32[64,7168]{1,0:T(8,128)S(1)}, u32[]{:S(2)}) %copy-start.1) | copy-done | bytes 1835032
  41.3 0.0 copy-start.3
  41.3 0.9 copy-done.3
  42.3 47.6 %elements.1.acc_ref = f32[64,7168]{1,0:T(8,128)} custom-call(s32[6,4096]{1,0:T(8,128)} %conn_ref.1, s32[8]{0:T(128)} %knots_ref.1, f32[4]{0:T(128)} %base_ref.1, f32[4,8]{1,0:T(4,128)} %slopes_ref.1, f32[64,7168]{1,0:T(8,128)} %copy-done.1, f32[32,56,128]{2,1,0:T(8,128)} %copy-done.3, f32[3,6,4096]{2,1,0:T(8,128)} %curl_ref.1, ...), custom_call_target="tpu_custom_call" | custom-call | tf_op jit(solution)/shard_map/elements/pallas_call | solution.py:314
  89.8 0.0 copy-start
  89.8 1.5 %copy-done = f32[64,7168]{1,0:T(8,128)S(1)} copy-done((f32[64,7168]{1,0:T(8,128)S(1)}, f32[64,7168]{1,0:T(8,128)}, u32[]{:S(2)}) %copy-start) | copy-done | bytes 1835032
  91.3 0.0 copy-start.6
  91.3 16.3 %combine.1 = (f32[16,5120]{1,0:T(8,128)S(1)}, f32[16,2048]{1,0:T(8,128)S(1)}) custom-call(f32[64,7168]{1,0:T(8,128)S(1)} %copy-done), custom_call_target="tpu_custom_call" | custom-call | tf_op jit(solution)/shard_map/combine/pallas_call | solution.py:392
  107.7 0.0 copy-done.6
  107.7 7.8 %finish.1 = f32[16,5120]{1,0:T(8,128)} custom-call(s32[2,1024]{1,0:T(2,128)S(1)} %copy-done.6, f32[16,5120]{1,0:T(8,128)S(1)} %get-tuple-element.11.own_ref, f32[16,2048]{1,0:T(8,128)S(1)} %get-tuple-element.12.ghost_ref), custom_call_target="tpu_custom_call" | custom-call | tf_op jit(solution)/shard_map/finish/pallas_call | solution.py:435
Async XLA Ops:
  0.0 1.4 %copy-start.2 = (f32[64,3,32,32]{0,3,2,1:T(8,128)S(1)}, f32[64,3,32,32]{0,3,2,1:T(8,128)}, u32[]{:S(2)}) copy-start(f32[64,3,32,32]{0,3,2,1:T(8,128)} %param.15) | copy-start | bytes 2359300
  1.4 1.0 copy-start.4
  2.4 0.7 copy-start.5
  3.1 0.7 copy-start.7
  40.1 1.2 %copy-start.1 = (f32[64,7168]{1,0:T(8,128)}, f32[64,7168]{1,0:T(8,128)S(1)}, u32[]{:S(2)}) copy-start(f32[64,7168]{1,0:T(8,128)S(1)} %get-tuple-element.9.ext_ref) | copy-start | bytes 5505028
  41.3 0.9 copy-start.3
  89.8 1.5 %copy-start = (f32[64,7168]{1,0:T(8,128)S(1)}, f32[64,7168]{1,0:T(8,128)}, u32[]{:S(2)}) copy-start(f32[64,7168]{1,0:T(8,128)} %elements.1.acc_ref) | copy-start | bytes 5505028
  91.3 16.3 %copy-start.6 = (s32[2,1024]{1,0:T(2,128)S(1)}, s32[2,1024]{1,0:T(2,128)}, u32[]{:S(2)}) copy-start(s32[2,1024]{1,0:T(2,128)} %faces_ref.3) | copy-start | bytes 24580
where the time goes:
time: 116 us; the launch traced here: 115 us
  Pallas kernels  108 us (93%)
  local copies, waits for them, and re-layouts  7.46 us (6%)
    pallas_call x1, Pallas kernels, elements(): pl.pallas_call(element_kernel, name='elements', out_shape=jax.ShapeDtypeS...  47.6 us
    pallas_call x1, Pallas kernels, spread(): pl.pallas_call(spread_kernel, name='spread', out_shape=(jax.ShapeDtypeStr...  36.3 us
    pallas_call x1, Pallas kernels, combine(): pl.pallas_call(combine_kernel, name='combine', out_shape=(jax.ShapeDtypeS...  16.3 us
    pallas_call x1, Pallas kernels, finish(): pl.pallas_call(finish_kernel, name='finish', out_shape=jax.ShapeDtypeStru...  7.78 us
    unnamed x16, local copies, waits for them, and re-layouts  7.46 us

commit v1 on v0

v1 whole, which is shorter than its diff:
```python
import functools

import numpy as np
import jax
import jax.numpy as jnp
from jax import lax
from jax.experimental import pallas as pl
from jax.experimental.pallas import tpu as pltpu
from jax.sharding import PartitionSpec as P

MESH = pl.DeviceIdType.MESH
N_MESH = 32
OWN = 5120
FACE = 1024
EXT = OWN + 2 * FACE
ROWS = 512
MSG = 56
PARTS = 4
CHUNK = OWN // PARTS


def block_diag_tables():
    length = 64
    t = np.arange(length)
    c = np.arange(length)
    freq = np.where(c < 32, c, c - 31)
    freq[-1] = 32
    sine = (c >= 32) & (c < 63)
    angle = 2.0 * np.pi * ((freq[:, None] * t[None, :]) % length) / length
    basis = np.where(sine[:, None], np.sin(angle), np.cos(angle))
    weight = np.where((c == 0) | (c == 63), 1.0 / length, 2.0 / length)
    inverse = np.kron(np.eye(2), basis)
    forward = np.kron(np.eye(2), (basis * weight[:, None]).T)
    return inverse.astype(np.float32), forward.astype(np.float32)


def forward_kernel(field_ref, point_ref, mat_ref, curl_ref, faces_ref, conn_ref, knots_ref, base_ref, slopes_ref,
                   inv_ref, fwd_ref, out_ref,
                   field, point, curl, opsend, op_in, field_t, face_rows, face_cols, ext, ext2, curl_t, wide, got, flux,
                   in_s, op_ss, op_rs, far_ss, far_rs, side_ss, side_rs, gh_ss, gh_rs, fw_ss, fw_rs, rel_ss, rel_rs):
    m = lax.axis_index("mesh")
    h = lax.axis_index("harm")
    up, down = lax.rem(m + 1, N_MESH), lax.rem(m + N_MESH - 1, N_MESH)
    side = h + 1 - 2 * lax.rem(h, 2)
    far = lax.rem(h + 2, 4)
    half = m // 16

    def block_of(source, target):
        crossing = (source // 16 + target // 16) % 2
        return lax.rem(h + 2 * crossing * lax.rem(source, 2), 4)

    load_field = pltpu.make_async_copy(field_ref, field, in_s.at[0])
    load_point = pltpu.make_async_copy(point_ref, point, in_s.at[1])
    load_curl = pltpu.make_async_copy(curl_ref, curl, in_s.at[2])
    load_field.start()
    load_point.start()
    load_curl.start()

    barrier = pltpu.get_barrier_semaphore()
    for peer in ((m, far), (m, side), (up, h), (down, h)):
        pl.semaphore_signal(barrier, inc=1, device_id=peer, device_id_type=MESH)

    @pl.loop(1, N_MESH)
    def _(d):
        source = lax.rem(m + N_MESH - d, N_MESH)
        pl.semaphore_signal(barrier, inc=1, device_id=(source, block_of(source, m)), device_id_type=MESH)

    load_field.wait()

    @pl.loop(0, OWN // 128, unroll=8)
    def _(b):
        at = pl.ds(pl.multiple_of(b * 128, 128), 128)
        field_t[at, :] = field[:, at].T

    pl.semaphore_wait(barrier, N_MESH - 1 + 4)

    def rows_of(who):
        return pl.ds(pl.multiple_of(16 * who, 16), 16)

    ghost_cols = pl.ds(OWN, 2 * FACE)

    def cols_of(c):
        return pl.ds(c * CHUNK, CHUNK)

    def own_copy(c, peer, ss, rs):
        return pltpu.make_async_remote_copy(
            src_ref=field.at[:, cols_of(c)], dst_ref=ext.at[rows_of(h), cols_of(c)],
            send_sem=ss.at[c], recv_sem=rs.at[c],
            device_id=(m, peer), device_id_type=MESH)

    to_far = [own_copy(c, far, far_ss, far_rs) for c in range(PARTS)]
    to_side = [own_copy(c, side, side_ss, side_rs) for c in range(PARTS)]
    for c in (*to_far, *to_side):
        c.start()
    keep = pltpu.make_async_copy(field, ext.at[rows_of(h), pl.ds(0, OWN)], in_s.at[3])
    keep.start()

    for f in range(2):
        @pl.loop(0, FACE // 16)
        def _(b):
            for k in range(16):
                n = faces_ref[f, b * 16 + k]
                face_rows[pl.ds(f * FACE + b * 16 + k, 1), :] = field_t[pl.ds(n, 1), :]

    @pl.loop(0, 2 * FACE // 128, unroll=8)
    def _(b):
        at = pl.ds(pl.multiple_of(b * 128, 128), 128)
        face_cols[:, at] = face_rows[at, :].T

    def ghost_copy(f, peer):
        return pltpu.make_async_remote_copy(
            src_ref=face_cols.at[:, pl.ds(f * FACE, FACE)],
            dst_ref=ext.at[rows_of(h), pl.ds(OWN + (1 - f) * FACE, FACE)],
            send_sem=gh_ss.at[f], recv_sem=gh_rs.at[f],
            device_id=(peer, h), device_id_type=MESH)

    ghosts = [ghost_copy(0, down), ghost_copy(1, up)]
    for c in ghosts:
        c.start()

    load_point.wait()

    @pl.loop(0, N_MESH)
    def _(p):
        for i in range(3):
            opsend[p, pl.ds(16 * i, 16), pl.ds(0, 64)] = point[i, p, pl.ds(0, 16), :]
            opsend[p, pl.ds(16 * i, 16), pl.ds(64, 64)] = point[i, p, pl.ds(16, 16), :]
        opsend[p, pl.ds(48, 8), :] = jnp.zeros((8, 128), jnp.float32)
        opsend[p, pl.ds(48, 1), pl.ds(0, 32)] = mat_ref[pl.ds(p, 1), :].astype(jnp.float32)

    def op_copy(d):
        p = lax.rem(m + d, N_MESH)
        target = lax.rem(h + 2 * ((half + p // 16) % 2) * lax.rem(m, 2), 4)
        return pltpu.make_async_remote_copy(
            src_ref=opsend.at[p], dst_ref=op_in.at[m],
            send_sem=op_ss.at[d], recv_sem=op_rs.at[d],
            device_id=(p, target), device_id_type=MESH)

    @pl.loop(1, N_MESH)
    def _(d):
        op_copy(d).start()
    op_keep = pltpu.make_async_copy(opsend.at[m], op_in.at[m], in_s.at[4])
    op_keep.start()

    for c in ghosts:
        c.wait_recv()

    def gfwd_copy(n, peer):
        return pltpu.make_async_remote_copy(
            src_ref=ext.at[rows_of(h), ghost_cols], dst_ref=ext.at[rows_of(h), ghost_cols],
            send_sem=fw_ss.at[n], recv_sem=fw_rs.at[n],
            device_id=(m, peer), device_id_type=MESH)

    gfar, gside = gfwd_copy(0, far), gfwd_copy(1, side)
    gfar.start()
    gside.start()

    def relay(c, cols):
        return pltpu.make_async_remote_copy(
            src_ref=ext.at[rows_of(far), cols], dst_ref=ext.at[rows_of(far), cols],
            send_sem=rel_ss.at[c], recv_sem=rel_rs.at[c],
            device_id=(m, side), device_id_type=MESH)

    relays = [relay(c, cols_of(c)) for c in range(PARTS)] + [relay(PARTS, ghost_cols)]

    low = lax.broadcasted_iota(jnp.int32, (16, 128), 1) < 64
    low1 = lax.broadcasted_iota(jnp.int32, (1, 128), 1) < 64

    load_curl.wait()

    @pl.loop(0, N_MESH, unroll=4)
    def _(s):
        at = pl.ds(pl.multiple_of(s * 128, 128), 128)
        pad = jnp.zeros((2, 128), jnp.float32)
        parts = []
        for i in range(3):
            parts += [curl[i, :, at], pad]
        curl_t[at, :] = jnp.concatenate(parts, axis=0).T

    for c in range(PARTS):
        @pl.loop(c * N_MESH // PARTS, (c + 1) * N_MESH // PARTS)
        def _(s):
            to = pl.ds(pl.multiple_of(s * 16, 16), 16)
            first = s * 128 + block_of(s, m) * 32
            c0 = curl_t[pl.ds(pl.multiple_of(first, 16), 16), :]
            c1 = curl_t[pl.ds(pl.multiple_of(first + 16, 16), 16), :]
            for i in range(3):
                for j in range(6):
                    col = i * 8 + j
                    wide[i * 6 + j, to, :] = jnp.where(low, jnp.broadcast_to(c0[:, col:col + 1], (16, 128)),
                                                       jnp.broadcast_to(c1[:, col:col + 1], (16, 128)))
        to_far[c].wait_recv()
        relays[c].start()
    gfar.wait_recv()
    relays[PARTS].start()

    keep.wait()
    for c in range(PARTS + 1):
        if c < PARTS:
            to_side[c].wait_recv()
        else:
            gside.wait_recv()
        relays[c].wait_recv()
        blocks = CHUNK // 128 if c < PARTS else 2 * FACE // 128

        @pl.loop(0, blocks, unroll=2)
        def _(b):
            at = pl.ds(pl.multiple_of(c * CHUNK + b * 128, 128), 128)
            x = ext[:, at]
            ext2[at, :] = jnp.concatenate([x, x], axis=0).T

    @pl.loop(0, N_MESH)
    def _(s):
        to = pl.ds(pl.multiple_of(s * 16, 16), 16)
        first = s * 128 + block_of(s, m) * 32
        for j in range(6):
            for k in range(16):
                a = ext2[pl.ds(conn_ref[j, first + k], 1), :]
                b = ext2[pl.ds(conn_ref[j, first + 16 + k], 1), :]
                got[pl.ds(j * 16 + k, 1), :] = jnp.where(low1, a, b)
        for i in range(3):
            s_i = wide[i * 6, to, :] * got[0:16, :]
            for j in range(1, 6):
                s_i = s_i + wide[i * 6 + j, to, :] * got[j * 16:(j + 1) * 16, :]
            flux[i, to, :] = s_i

    @pl.loop(1, N_MESH)
    def _(d):
        op_copy(d).wait_recv()

    op_keep.wait()
    growth = [jnp.exp(jnp.float32(-0.5) * knots_ref[k].astype(jnp.float32)) for k in range(8)]

    @pl.loop(0, ROWS // 64)
    def _(r):
        to = pl.ds(pl.multiple_of(r * 64, 64), 64)
        f = [jnp.dot(flux[i, to, :], inv_ref[...], precision=lax.Precision.HIGHEST,
                     preferred_element_type=jnp.float32) for i in range(3)]
        b = [jnp.concatenate([op_in[r * 4 + s, 16 * i:16 * i + 16, :] for s in range(4)], axis=0)
             for i in range(3)]
        kinds = []
        for s in range(4):
            mt = jnp.broadcast_to(op_in[r * 4 + s, pl.ds(48, 1), :], (8, 128)).T
            kinds.append(jnp.where(low, jnp.broadcast_to(mt[0:16, 0:1], (16, 128)),
                                   jnp.broadcast_to(mt[16:32, 0:1], (16, 128))))
        mat = jnp.concatenate(kinds, axis=0)

        def pick(values):
            x = jnp.where(mat == 1.0, values[1], values[0])
            x = jnp.where(mat == 2.0, values[2], x)
            return jnp.where(mat == 3.0, values[3], x)

        q = b[0] * b[0] + b[1] * b[1] + b[2] * b[2]
        u = jnp.exp(2.0 * q)
        nu = pick([base_ref[a] for a in range(4)])
        dnu = jnp.zeros_like(q)
        for k in range(8):
            slope = pick([slopes_ref[a, k] for a in range(4)])
            e = u * growth[k]
            w = 1.0 + e
            nu = nu + slope * jnp.log(w)
            dnu = dnu + slope * (e / w)
        proj = b[0] * f[0] + b[1] * f[1] + b[2] * f[2]
        scale = 4.0 * dnu * proj
        f = [jnp.dot(nu * f[i] + scale * b[i], fwd_ref[...], precision=lax.Precision.HIGHEST,
                     preferred_element_type=jnp.float32) for i in range(3)]
        for j in range(6):
            out_ref[pl.ds(pl.multiple_of(j * ROWS + r * 64, 64), 64), :] = (
                wide[j, to, :] * f[0] + wide[6 + j, to, :] * f[1] + wide[12 + j, to, :] * f[2])

    for c in (*to_far, *to_side, *ghosts, gfar, gside, *relays):
        c.wait_send()

    @pl.loop(1, N_MESH)
    def _(d):
        op_copy(d).wait_send()


def forward(field, point, material, curl, faces, conn, knots, base, slopes):
    inverse, forward_table = block_diag_tables()
    smem = pl.BlockSpec(memory_space=pltpu.SMEM)
    vmem = pl.BlockSpec(memory_space=pltpu.VMEM)
    hbm = pl.BlockSpec(memory_space=pl.ANY)
    f32 = jnp.float32
    dma = pltpu.SemaphoreType.DMA
    return pl.pallas_call(
        forward_kernel,
        name="forward",
        out_shape=jax.ShapeDtypeStruct((6 * ROWS, 128), f32),
        in_specs=[hbm, hbm, vmem, hbm, smem, smem, smem, smem, smem, vmem, vmem],
        out_specs=vmem,
        scratch_shapes=[
            pltpu.VMEM((16, OWN), f32), pltpu.VMEM((3, 32, 32, 64), f32), pltpu.VMEM((3, 6, 4096), f32),
            pltpu.VMEM((N_MESH, MSG, 128), f32), pltpu.VMEM((N_MESH, MSG, 128), f32),
            pltpu.VMEM((OWN, 16), f32), pltpu.VMEM((2 * FACE, 16), f32), pltpu.VMEM((16, 2 * FACE), f32),
            pltpu.VMEM((64, EXT), f32), pltpu.VMEM((EXT, 128), f32), pltpu.VMEM((4096, 24), f32),
            pltpu.VMEM((18, ROWS, 128), f32), pltpu.VMEM((96, 128), f32), pltpu.VMEM((3, ROWS, 128), f32),
            dma((5,)), dma((N_MESH,)), dma((N_MESH,)), dma((PARTS,)), dma((PARTS,)), dma((PARTS,)), dma((PARTS,)),
            dma((2,)), dma((2,)), dma((2,)), dma((2,)), dma((PARTS + 1,)), dma((PARTS + 1,)),
        ],
        compiler_params=pltpu.CompilerParams(collective_id=0, has_side_effects=True,
                                             vmem_limit_bytes=60 << 20),
    )(field, point, material, curl, faces, conn, knots, base, slopes, jnp.asarray(inverse), jnp.asarray(forward_table))


def scatter_kernel(conn_ref, con_ref, out_ref, acc0, acc1, acc2, acc3):
    m = lax.axis_index("mesh")
    h = lax.axis_index("harm")
    accs = (acc0, acc1, acc2, acc3)
    low = lax.broadcasted_iota(jnp.int32, (64, 128), 1) < 64

    def block_of(source, target):
        crossing = (source // 16 + target // 16) % 2
        return lax.rem(h + 2 * crossing * lax.rem(source, 2), 4)

    @pl.loop(0, EXT // 64)
    def _(b):
        at = pl.ds(pl.multiple_of(b * 64, 64), 64)
        for a in accs:
            a[at, :] = jnp.zeros((64, 128), jnp.float32)

    @pl.loop(0, N_MESH)
    def _(s):
        first = s * 128 + block_of(s, m) * 32
        for k in range(16):
            for j in range(6):
                row = con_ref[pl.ds(j * ROWS + s * 16 + k, 1), :]
                n0 = conn_ref[j, first + k]
                n1 = conn_ref[j, first + 16 + k]
                a0, a1 = accs[j % 2], accs[2 + j % 2]
                a0[pl.ds(n0, 1), :] = a0[pl.ds(n0, 1), :] + row
                a1[pl.ds(n1, 1), :] = a1[pl.ds(n1, 1), :] + row

    @pl.loop(0, EXT // 64, unroll=2)
    def _(b):
        at = pl.ds(pl.multiple_of(b * 64, 64), 64)
        out_ref[at, :] = jnp.where(low, acc0[at, :] + acc1[at, :], acc2[at, :] + acc3[at, :])


def scatter(conn, con):
    vmem = pl.BlockSpec(memory_space=pltpu.VMEM)
    big = pltpu.VMEM((EXT, 128), jnp.float32)
    return pl.pallas_call(
        scatter_kernel,
        name="scatter",
        out_shape=jax.ShapeDtypeStruct((EXT, 128), jnp.float32),
        in_specs=[pl.BlockSpec(memory_space=pltpu.SMEM), vmem],
        out_specs=vmem,
        scratch_shapes=[big, big, big, big],
        compiler_params=pltpu.CompilerParams(vmem_limit_bytes=32 << 20),
    )(conn, con)


def combine_kernel(rows_ref, own_out, ghost_out, acc, pairs, summed, zin, ghost_sum, ghost_in,
                   p_ss, p_rs, z_ss, z_rs, g_ss, g_rs):
    m = lax.axis_index("mesh")
    h = lax.axis_index("harm")
    up, down = lax.rem(m + 1, N_MESH), lax.rem(m + N_MESH - 1, N_MESH)
    side = h + 1 - 2 * lax.rem(h, 2)
    far = lax.rem(h + 2, 4)
    cross = lax.rem(side + 2, 4)
    barrier = pltpu.get_barrier_semaphore()
    for peer in ((m, side), (m, far), (up, h), (down, h)):
        pl.semaphore_signal(barrier, inc=1, device_id=peer, device_id_type=MESH)

    bounds = [(OWN, 2 * FACE)] + [(c * CHUNK, CHUNK) for c in range(PARTS)]
    chunks = [pl.ds(a, n) for a, n in bounds]

    def block(who):
        return pl.ds(pl.multiple_of(16 * who, 16), 16)

    def turn(c):
        start, n = bounds[c]

        @pl.loop(0, n // 128, unroll=2)
        def _(b):
            at = pl.ds(pl.multiple_of(start + b * 128, 128), 128)
            x = rows_ref[at, :].T
            acc[:, at] = x[0:64, :] + x[64:128, :]

    def pair_copy(c, n):
        return pltpu.make_async_remote_copy(
            src_ref=acc.at[block((side, cross)[n]), chunks[c]], dst_ref=pairs.at[n, :, chunks[c]],
            send_sem=p_ss.at[c, n], recv_sem=p_rs.at[c, n],
            device_id=(m, side), device_id_type=MESH)

    def z_copy(c):
        return pltpu.make_async_remote_copy(
            src_ref=summed.at[:, chunks[c]], dst_ref=zin.at[:, chunks[c]],
            send_sem=z_ss.at[c], recv_sem=z_rs.at[c],
            device_id=(m, far), device_id_type=MESH)

    def g_copy(f, peer):
        return pltpu.make_async_remote_copy(
            src_ref=ghost_sum.at[:, pl.ds(f * FACE, FACE)],
            dst_ref=ghost_in.at[:, pl.ds((1 - f) * FACE, FACE)],
            send_sem=g_ss.at[f], recv_sem=g_rs.at[f],
            device_id=(peer, h), device_id_type=MESH)

    count = PARTS + 1
    far_pairs = [pair_copy(c, 1) for c in range(count)]
    own_pairs = [pair_copy(c, 0) for c in range(count)]
    zs = [z_copy(c) for c in range(count)]
    gs = [g_copy(0, down), g_copy(1, up)]

    turn(0)
    pl.semaphore_wait(barrier, 4)
    far_pairs[0].start()
    own_pairs[0].start()
    for c in range(count):
        if c + 1 < count:
            turn(c + 1)
            far_pairs[c + 1].start()
            own_pairs[c + 1].start()
        far_pairs[c].wait_recv()
        summed[:, chunks[c]] = acc[block(far), chunks[c]] + pairs[1, :, chunks[c]]
        zs[c].start()

    def total(c):
        own_pairs[c].wait_recv()
        zs[c].wait_recv()
        return acc[block(h), chunks[c]] + pairs[0, :, chunks[c]] + zin[:, chunks[c]]

    ghost_sum[...] = total(0)
    for g in gs:
        g.start()
    for c in range(1, count):
        own_out[:, chunks[c]] = total(c)
    for g in gs:
        g.wait_recv()
    ghost_out[...] = ghost_in[...]
    for c in (*far_pairs, *own_pairs, *zs, *gs):
        c.wait_send()


def combine(rows):
    vmem = pl.BlockSpec(memory_space=pltpu.VMEM)
    dma = pltpu.SemaphoreType.DMA
    f32 = jnp.float32
    return pl.pallas_call(
        combine_kernel,
        name="combine",
        out_shape=(jax.ShapeDtypeStruct((16, OWN), f32), jax.ShapeDtypeStruct((16, 2 * FACE), f32)),
        in_specs=[vmem],
        out_specs=(vmem, vmem),
        scratch_shapes=[
            pltpu.VMEM((64, EXT), f32), pltpu.VMEM((2, 16, EXT), f32), pltpu.VMEM((16, EXT), f32),
            pltpu.VMEM((16, EXT), f32), pltpu.VMEM((16, 2 * FACE), f32), pltpu.VMEM((16, 2 * FACE), f32),
            dma((PARTS + 1, 2)), dma((PARTS + 1, 2)), dma((PARTS + 1,)), dma((PARTS + 1,)), dma((2,)), dma((2,)),
        ],
        compiler_params=pltpu.CompilerParams(collective_id=1, has_side_effects=True,
                                             vmem_limit_bytes=32 << 20),
    )(rows)


def finish_kernel(faces_ref, own_ref, ghost_ref, out_ref, ghost_t, full_t):
    @pl.loop(0, OWN // 128, unroll=8)
    def _(b):
        full_t[pl.ds(pl.multiple_of(b * 128, 128), 128), :] = jnp.zeros((128, 16), jnp.float32)

    @pl.loop(0, 2 * FACE // 128, unroll=8)
    def _(b):
        at = pl.ds(pl.multiple_of(b * 128, 128), 128)
        ghost_t[at, :] = ghost_ref[:, at].T

    for f in range(2):
        @pl.loop(0, FACE // 16)
        def _(b):
            for k in range(16):
                full_t[pl.ds(faces_ref[f, b * 16 + k], 1), :] = ghost_t[pl.ds(f * FACE + b * 16 + k, 1), :]

    @pl.loop(0, OWN // 128, unroll=8)
    def _(b):
        at = pl.ds(pl.multiple_of(b * 128, 128), 128)
        out_ref[:, at] = own_ref[:, at] + full_t[at, :].T


def finish(faces, own, ghost):
    vmem = pl.BlockSpec(memory_space=pltpu.VMEM)
    return pl.pallas_call(
        finish_kernel,
        name="finish",
        out_shape=jax.ShapeDtypeStruct((16, OWN), jnp.float32),
        in_specs=[pl.BlockSpec(memory_space=pltpu.SMEM), vmem, vmem],
        out_specs=vmem,
        scratch_shapes=[pltpu.VMEM((2 * FACE, 16), jnp.float32), pltpu.VMEM((OWN, 16), jnp.float32)],
        compiler_params=pltpu.CompilerParams(vmem_limit_bytes=40 << 20),
    )(faces, own, ghost)


def per_device(field_in, faces, connectivity, curl_vectors, operating_point, material, bh_knots, curve_base,
               curve_slopes):
    point = jnp.transpose(operating_point, (1, 2, 3, 0))
    contributions = forward(field_in, point, material, curl_vectors, faces, connectivity, bh_knots, curve_base,
                            curve_slopes)
    own, ghost = combine(scatter(connectivity, contributions))
    return finish(faces, own, ghost)


def solution(mesh):
    return jax.shard_map(
        per_device,
        mesh=mesh,
        in_specs=(P("harm", "mesh"), P(None, "mesh"), P(None, "mesh"), P(None, None, "mesh"),
                  P(None, None, None, ("mesh", "harm")), P(None, ("mesh", "harm")), P(), P(), P()),
        out_specs=P("harm", "mesh"),
        check_vma=False,
    )
```

time: 116 us -> 95 us (0.82)
  Pallas kernels: 108 us -> 93.3 us
  local copies, waits for them, and re-layouts: 7.46 us -> 1.41 us
    pallas_call x2, Pallas kernels: 83.8 us -> 67.1 us  [the longest x1 53.7 us: forward(): pl.pallas_call(forward_kernel, name='forward', out_shape=jax.ShapeDtypeSt...]
    unnamed x16 -> x6, local copies, waits for them, and re-layouts: 7.46 us -> 1.41 us
    pallas_call x1, Pallas kernels: 16.3 us -> 18.7 us  [combine(): pl.pallas_call(combine_kernel, name='combine', out_shape=(jax.ShapeDtypeS...]
where the time goes in v1:
time: 95 us; the launch traced here: 94.8 us
  Pallas kernels  93.3 us (98%)
  local copies, waits for them, and re-layouts  1.41 us (1%)
    pallas_call x1, Pallas kernels, forward(): pl.pallas_call(forward_kernel, name='forward', out_shape=jax.ShapeDtypeSt...  53.7 us
    pallas_call x1, Pallas kernels, combine(): pl.pallas_call(combine_kernel, name='combine', out_shape=(jax.ShapeDtypeS...  18.7 us
    pallas_call x1, Pallas kernels, scatter(): pl.pallas_call(scatter_kernel, name='scatter', out_shape=jax.ShapeDtypeSt...  13.5 us
    pallas_call x1, Pallas kernels, finish(): pl.pallas_call(finish_kernel, name='finish', out_shape=jax.ShapeDtypeStru...  7.46 us

profile of v1, /device:TPU:1, one launch (start us, length us, event | category | flops | bytes accessed | tf_op | source)
XLA Modules:
  0.0 94.8 jit_solution(6448305697023615271)
XLA Ops:
  0.0 0.0 copy-start.1
  0.0 53.7 %forward.1.con_ref = f32[3072,128]{1,0:T(8,128)} custom-call(f32[16,5120]{1,0:T(8,128)} %field_ref.1, f32[3,32,32,64]{3,2,1,0:T(8,128)} %bitcast.1, s32[32,32]{1,0:T(8,128)} %mat_ref.1, f32[3,6,4096]{2,1,0:T(8,128)} %curl_ref.1, s32[2,1024]{1,0:T(2,128)} %faces_ref.3, s32[6,4096]{1,0:T(8,128)} %conn_ref.3, s32[8]{0:T(128)} %knots_ref.1, f32[4]{0:T(128)} %base_ref.1, ...), custom_call_target="tpu_custom_call" | custom-call | tf_op jit(solution)/shard_map/forward/pallas_call | solution.py:286
  53.7 0.0 copy-done.1
  53.7 0.0 copy-start
  53.7 1.4 %copy-done = f32[3072,128]{1,0:T(8,128)S(1)} copy-done((f32[3072,128]{1,0:T(8,128)S(1)}, f32[3072,128]{1,0:T(8,128)}, u32[]{:S(2)}) %copy-start) | copy-done | bytes 1572888
  55.1 13.5 %scatter.1.rows_ref = f32[7168,128]{1,0:T(8,128)S(1)} custom-call(s32[6,4096]{1,0:T(8,128)S(1)} %copy-done.1, f32[3072,128]{1,0:T(8,128)S(1)} %copy-done), custom_call_target="tpu_custom_call" | custom-call | tf_op jit(solution)/shard_map/scatter/pallas_call | solution.py:343
  68.6 0.0 copy-start.2
  68.6 18.7 %combine.1 = (f32[16,5120]{1,0:T(8,128)S(1)}, f32[16,2048]{1,0:T(8,128)S(1)}) custom-call(f32[7168,128]{1,0:T(8,128)S(1)} %scatter.1.rows_ref), custom_call_target="tpu_custom_call" | custom-call | tf_op jit(solution)/shard_map/combine/pallas_call | solution.py:440
  87.3 0.0 copy-done.2
  87.3 7.5 %finish.1 = f32[16,5120]{1,0:T(8,128)} custom-call(s32[2,1024]{1,0:T(2,128)S(1)} %copy-done.2, f32[16,5120]{1,0:T(8,128)S(1)} %get-tuple-element.7.own_ref, f32[16,2048]{1,0:T(8,128)S(1)} %get-tuple-element.8.ghost_ref), custom_call_target="tpu_custom_call" | custom-call | tf_op jit(solution)/shard_map/finish/pallas_call | solution.py:480
Async XLA Ops:
  0.0 53.7 %copy-start.1 = (s32[6,4096]{1,0:T(8,128)S(1)}, s32[6,4096]{1,0:T(8,128)}, u32[]{:S(2)}) copy-start(s32[6,4096]{1,0:T(8,128)} %conn_ref.3) | copy-start | bytes 294916
  53.7 1.4 %copy-start = (f32[3072,128]{1,0:T(8,128)S(1)}, f32[3072,128]{1,0:T(8,128)}, u32[]{:S(2)}) copy-start(f32[3072,128]{1,0:T(8,128)} %forward.1.con_ref) | copy-start | bytes 4718596
  68.6 18.7 %copy-start.2 = (s32[2,1024]{1,0:T(2,128)S(1)}, s32[2,1024]{1,0:T(2,128)}, u32[]{:S(2)}) copy-start(s32[2,1024]{1,0:T(2,128)} %faces_ref.3) | copy-start | bytes 24580

commit v2 on v1

--- a/solution.py
+++ b/solution.py
@@ -34,10 +34,10 @@
     return inverse.astype(np.float32), forward.astype(np.float32)
 
 
-def forward_kernel(field_ref, point_ref, mat_ref, curl_ref, faces_ref, conn_ref, knots_ref, base_ref, slopes_ref,
+def forward_kernel(field_ref, point_ref, mat_ref, curl_ref, faces_hbm, conn_hbm, knots_ref, base_ref, slopes_ref,
                    inv_ref, fwd_ref, out_ref,
-                   field, point, curl, opsend, op_in, field_t, face_rows, face_cols, ext, ext2, curl_t, wide, got, flux,
-                   in_s, op_ss, op_rs, far_ss, far_rs, side_ss, side_rs, gh_ss, gh_rs, fw_ss, fw_rs, rel_ss, rel_rs):
+                   field, point, curl, opsend, op_in, field_t, face_rows, face_cols, ext, ext2, curl_t, wide, got, flux, faces_ref, conn_ref,
+                   in_s, op_ss, op_rs, far_ss, far_rs, side_ss, side_rs, gh_ss, gh_rs, fw_ss, fw_rs, rel_ss, rel_rs, idx_s):
     m = lax.axis_index("mesh")
     h = lax.axis_index("harm")
     up, down = lax.rem(m + 1, N_MESH), lax.rem(m + N_MESH - 1, N_MESH)
@@ -55,6 +55,12 @@
     load_field.start()
     load_point.start()
     load_curl.start()
+    load_faces = [pltpu.make_async_copy(faces_hbm.at[f], faces_ref.at[pl.ds(f * FACE, FACE)], idx_s.at[f])
+                  for f in range(2)]
+    load_conn = [pltpu.make_async_copy(conn_hbm.at[j], conn_ref.at[pl.ds(j * 4096, 4096)], idx_s.at[2 + j])
+                 for j in range(6)]
+    for c in (*load_faces, *load_conn):
+        c.start()
 
     barrier = pltpu.get_barrier_semaphore()
     for peer in ((m, far), (m, side), (up, h), (down, h)):
@@ -95,12 +101,15 @@
     keep = pltpu.make_async_copy(field, ext.at[rows_of(h), pl.ds(0, OWN)], in_s.at[3])
     keep.start()
 
-    for f in range(2):
-        @pl.loop(0, FACE // 16)
-        def _(b):
-            for k in range(16):
-                n = faces_ref[f, b * 16 + k]
-                face_rows[pl.ds(f * FACE + b * 16 + k, 1), :] = field_t[pl.ds(n, 1), :]
+    for c in load_faces:
+        c.wait()
+
+    @pl.loop(0, 2 * FACE // 32)
+    def _(b):
+        near = faces_ref.at[pl.ds(pl.multiple_of(b * 32, 32), 32)]
+        to = face_rows.at[pl.ds(pl.multiple_of(b * 32, 32), 32), :]
+        for k in range(32):
+            to[pl.ds(k, 1), :] = field_t[pl.ds(near[k], 1), :]
 
     @pl.loop(0, 2 * FACE // 128, unroll=8)
     def _(b):
@@ -194,6 +203,8 @@
     gfar.wait_recv()
     relays[PARTS].start()
 
+    for c in load_conn:
+        c.wait()
     keep.wait()
     for c in range(PARTS + 1):
         if c < PARTS:
@@ -212,11 +223,12 @@
     @pl.loop(0, N_MESH)
     def _(s):
         to = pl.ds(pl.multiple_of(s * 16, 16), 16)
-        first = s * 128 + block_of(s, m) * 32
+        first = pl.multiple_of(s * 128 + block_of(s, m) * 32, 32)
+        near = conn_ref.at[pl.ds(first, 5 * 4096 + 32)]
         for j in range(6):
             for k in range(16):
-                a = ext2[pl.ds(conn_ref[j, first + k], 1), :]
-                b = ext2[pl.ds(conn_ref[j, first + 16 + k], 1), :]
+                a = ext2[pl.ds(near[j * 4096 + k], 1), :]
+                b = ext2[pl.ds(near[j * 4096 + 16 + k], 1), :]
                 got[pl.ds(j * 16 + k, 1), :] = jnp.where(low1, a, b)
         for i in range(3):
             s_i = wide[i * 6, to, :] * got[0:16, :]
@@ -287,7 +299,7 @@
         forward_kernel,
         name="forward",
         out_shape=jax.ShapeDtypeStruct((6 * ROWS, 128), f32),
-        in_specs=[hbm, hbm, vmem, hbm, smem, smem, smem, smem, smem, vmem, vmem],
+        in_specs=[hbm, hbm, vmem, hbm, hbm, hbm, smem, smem, smem, vmem, vmem],
         out_specs=vmem,
         scratch_shapes=[
             pltpu.VMEM((16, OWN), f32), pltpu.VMEM((3, 32, 32, 64), f32), pltpu.VMEM((3, 6, 4096), f32),
@@ -295,46 +307,55 @@
             pltpu.VMEM((OWN, 16), f32), pltpu.VMEM((2 * FACE, 16), f32), pltpu.VMEM((16, 2 * FACE), f32),
             pltpu.VMEM((64, EXT), f32), pltpu.VMEM((EXT, 128), f32), pltpu.VMEM((4096, 24), f32),
             pltpu.VMEM((18, ROWS, 128), f32), pltpu.VMEM((96, 128), f32), pltpu.VMEM((3, ROWS, 128), f32),
+            pltpu.SMEM((2 * FACE,), jnp.int32), pltpu.SMEM((6 * 4096,), jnp.int32),
             dma((5,)), dma((N_MESH,)), dma((N_MESH,)), dma((PARTS,)), dma((PARTS,)), dma((PARTS,)), dma((PARTS,)),
-            dma((2,)), dma((2,)), dma((2,)), dma((2,)), dma((PARTS + 1,)), dma((PARTS + 1,)),
+            dma((2,)), dma((2,)), dma((2,)), dma((2,)), dma((PARTS + 1,)), dma((PARTS + 1,)), dma((8,)),
         ],
         compiler_params=pltpu.CompilerParams(collective_id=0, has_side_effects=True,
                                              vmem_limit_bytes=60 << 20),
     )(field, point, material, curl, faces, conn, knots, base, slopes, jnp.asarray(inverse), jnp.asarray(forward_table))
 
 
-def scatter_kernel(conn_ref, con_ref, out_ref, acc0, acc1, acc2, acc3):
+def scatter_kernel(conn_hbm, con_ref, out_ref, acc0, acc1, acc2, acc3, acc4, acc5, conn_ref, sem):
     m = lax.axis_index("mesh")
     h = lax.axis_index("harm")
-    accs = (acc0, acc1, acc2, acc3)
+    accs = (acc0, acc1, acc2, acc3, acc4, acc5)
     low = lax.broadcasted_iota(jnp.int32, (64, 128), 1) < 64
 
     def block_of(source, target):
         crossing = (source // 16 + target // 16) % 2
         return lax.rem(h + 2 * crossing * lax.rem(source, 2), 4)
 
+    loads = [pltpu.make_async_copy(conn_hbm.at[j], conn_ref.at[pl.ds(j * 4096, 4096)], sem.at[j]) for j in range(6)]
+    for c in loads:
+        c.start()
+
     @pl.loop(0, EXT // 64)
     def _(b):
         at = pl.ds(pl.multiple_of(b * 64, 64), 64)
         for a in accs:
             a[at, :] = jnp.zeros((64, 128), jnp.float32)
 
+    for c in loads:
+        c.wait()
+
     @pl.loop(0, N_MESH)
     def _(s):
-        first = s * 128 + block_of(s, m) * 32
+        first = pl.multiple_of(s * 128 + block_of(s, m) * 32, 32)
+        near = conn_ref.at[pl.ds(first, 5 * 4096 + 32)]
         for k in range(16):
             for j in range(6):
                 row = con_ref[pl.ds(j * ROWS + s * 16 + k, 1), :]
-                n0 = conn_ref[j, first + k]
-                n1 = conn_ref[j, first + 16 + k]
-                a0, a1 = accs[j % 2], accs[2 + j % 2]
+                n0 = near[j * 4096 + k]
+                n1 = near[j * 4096 + 16 + k]
+                a0, a1 = accs[j % 3], accs[3 + j % 3]
                 a0[pl.ds(n0, 1), :] = a0[pl.ds(n0, 1), :] + row
                 a1[pl.ds(n1, 1), :] = a1[pl.ds(n1, 1), :] + row
 
     @pl.loop(0, EXT // 64, unroll=2)
     def _(b):
         at = pl.ds(pl.multiple_of(b * 64, 64), 64)
-        out_ref[at, :] = jnp.where(low, acc0[at, :] + acc1[at, :], acc2[at, :] + acc3[at, :])
+        out_ref[at, :] = jnp.where(low, acc0[at, :] + acc1[at, :] + acc2[at, :], acc3[at, :] + acc4[at, :] + acc5[at, :])
 
 
 def scatter(conn, con):
@@ -344,9 +365,9 @@
         scatter_kernel,
         name="scatter",
         out_shape=jax.ShapeDtypeStruct((EXT, 128), jnp.float32),
-        in_specs=[pl.BlockSpec(memory_space=pltpu.SMEM), vmem],
+        in_specs=[pl.BlockSpec(memory_space=pl.ANY), vmem],
         out_specs=vmem,
-        scratch_shapes=[big, big, big, big],
+        scratch_shapes=[big, big, big, big, big, big, pltpu.SMEM((6 * 4096,), jnp.int32), pltpu.SemaphoreType.DMA((6,))],
         compiler_params=pltpu.CompilerParams(vmem_limit_bytes=32 << 20),
     )(conn, con)
 
@@ -453,7 +474,12 @@
     )(rows)
 
 
-def finish_kernel(faces_ref, own_ref, ghost_ref, out_ref, ghost_t, full_t):
+def finish_kernel(faces_hbm, own_ref, ghost_ref, out_ref, ghost_t, full_t, faces_ref, idx_s):
+    loads = [pltpu.make_async_copy(faces_hbm.at[f], faces_ref.at[pl.ds(f * FACE, FACE)], idx_s.at[f])
+             for f in range(2)]
+    for c in loads:
+        c.start()
+
     @pl.loop(0, OWN // 128, unroll=8)
     def _(b):
         full_t[pl.ds(pl.multiple_of(b * 128, 128), 128), :] = jnp.zeros((128, 16), jnp.float32)
@@ -463,11 +489,15 @@
         at = pl.ds(pl.multiple_of(b * 128, 128), 128)
         ghost_t[at, :] = ghost_ref[:, at].T
 
-    for f in range(2):
-        @pl.loop(0, FACE // 16)
-        def _(b):
-            for k in range(16):
-                full_t[pl.ds(faces_ref[f, b * 16 + k], 1), :] = ghost_t[pl.ds(f * FACE + b * 16 + k, 1), :]
+    for c in loads:
+        c.wait()
+
+    @pl.loop(0, 2 * FACE // 32)
+    def _(b):
+        near = faces_ref.at[pl.ds(pl.multiple_of(b * 32, 32), 32)]
+        rows = ghost_t.at[pl.ds(pl.multiple_of(b * 32, 32), 32), :]
+        for k in range(32):
+            full_t[pl.ds(near[k], 1), :] = rows[pl.ds(k, 1), :]
 
     @pl.loop(0, OWN // 128, unroll=8)
     def _(b):
@@ -481,9 +511,10 @@
         finish_kernel,
         name="finish",
         out_shape=jax.ShapeDtypeStruct((16, OWN), jnp.float32),
-        in_specs=[pl.BlockSpec(memory_space=pltpu.SMEM), vmem, vmem],
+        in_specs=[pl.BlockSpec(memory_space=pl.ANY), vmem, vmem],
         out_specs=vmem,
-        scratch_shapes=[pltpu.VMEM((2 * FACE, 16), jnp.float32), pltpu.VMEM((OWN, 16), jnp.float32)],
+        scratch_shapes=[pltpu.VMEM((2 * FACE, 16), jnp.float32), pltpu.VMEM((OWN, 16), jnp.float32),
+                        pltpu.SMEM((2 * FACE,), jnp.int32), pltpu.SemaphoreType.DMA((2,))],
         compiler_params=pltpu.CompilerParams(vmem_limit_bytes=40 << 20),
     )(faces, own, ghost)
 

time: 95 us -> 79.6 us (0.84)
  Pallas kernels: 93.3 us -> 78 us
    pallas_call x1, Pallas kernels: 53.7 us -> 46.1 us  [forward(): pl.pallas_call(forward_kernel, name='forward', out_shape=jax.ShapeDtypeSt...]
    pallas_call x1, Pallas kernels: 13.5 us -> 9.59 us  [scatter(): pl.pallas_call(scatter_kernel, name='scatter', out_shape=jax.ShapeDtypeSt...]
    pallas_call x1, Pallas kernels: 7.46 us -> 4.26 us  [finish(): pl.pallas_call(finish_kernel, name='finish', out_shape=jax.ShapeDtypeStru...]
where the time goes in v2:
time: 79.6 us; the launch traced here: 79.5 us
  Pallas kernels  78 us (98%)
  local copies, waits for them, and re-layouts  1.41 us (2%)
    pallas_call x1, Pallas kernels, forward(): pl.pallas_call(forward_kernel, name='forward', out_shape=jax.ShapeDtypeSt...  46.1 us
    pallas_call x1, Pallas kernels, combine(): pl.pallas_call(combine_kernel, name='combine', out_shape=(jax.ShapeDtypeS...  18 us
    pallas_call x1, Pallas kernels, scatter(): pl.pallas_call(scatter_kernel, name='scatter', out_shape=jax.ShapeDtypeSt...  9.59 us
    pallas_call x1, Pallas kernels, finish(): pl.pallas_call(finish_kernel, name='finish', out_shape=jax.ShapeDtypeStru...  4.26 us

profile of v2, /device:TPU:1, one launch (start us, length us, event | category | flops | bytes accessed | tf_op | source)
XLA Modules:
  0.0 79.5 jit_solution(14682980864867890477)
XLA Ops:
  0.0 0.0 copy-start.1
  0.0 46.1 %forward.1.con_ref = f32[3072,128]{1,0:T(8,128)} custom-call(f32[16,5120]{1,0:T(8,128)} %field_ref.1, f32[3,32,32,64]{3,2,1,0:T(8,128)} %bitcast.1, s32[32,32]{1,0:T(8,128)} %mat_ref.1, f32[3,6,4096]{2,1,0:T(8,128)} %curl_ref.1, s32[2,1024]{1,0:T(2,128)} %faces_hbm.3, s32[6,4096]{1,0:T(8,128)} %conn_hbm.3, s32[8]{0:T(128)} %knots_ref.1, f32[4]{0:T(128)} %base_ref.1, ...), custom_call_target="tpu_custom_call" | custom-call | tf_op jit(solution)/shard_map/forward/pallas_call | solution.py:298
  46.2 0.0 copy-done.1
  46.2 0.0 copy-start
  46.2 1.4 %copy-done = f32[3072,128]{1,0:T(8,128)S(1)} copy-done((f32[3072,128]{1,0:T(8,128)S(1)}, f32[3072,128]{1,0:T(8,128)}, u32[]{:S(2)}) %copy-start) | copy-done | bytes 1572888
  47.6 9.6 %scatter.1.rows_ref = f32[7168,128]{1,0:T(8,128)S(1)} custom-call(s32[6,4096]{1,0:T(8,128)S(1)} %copy-done.1, f32[3072,128]{1,0:T(8,128)S(1)} %copy-done), custom_call_target="tpu_custom_call" | custom-call | tf_op jit(solution)/shard_map/scatter/pallas_call | solution.py:364
  57.2 0.0 copy-start.2
  57.2 18.0 %combine.1 = (f32[16,5120]{1,0:T(8,128)S(1)}, f32[16,2048]{1,0:T(8,128)S(1)}) custom-call(f32[7168,128]{1,0:T(8,128)S(1)} %scatter.1.rows_ref), custom_call_target="tpu_custom_call" | custom-call | tf_op jit(solution)/shard_map/combine/pallas_call | solution.py:461
  75.2 0.0 copy-done.2
  75.2 4.3 %finish.1 = f32[16,5120]{1,0:T(8,128)} custom-call(s32[2,1024]{1,0:T(2,128)S(1)} %copy-done.2, f32[16,5120]{1,0:T(8,128)S(1)} %get-tuple-element.7.own_ref, f32[16,2048]{1,0:T(8,128)S(1)} %get-tuple-element.8.ghost_ref), custom_call_target="tpu_custom_call" | custom-call | tf_op jit(solution)/shard_map/finish/pallas_call | solution.py:510
Async XLA Ops:
  0.0 46.2 %copy-start.1 = (s32[6,4096]{1,0:T(8,128)S(1)}, s32[6,4096]{1,0:T(8,128)}, u32[]{:S(2)}) copy-start(s32[6,4096]{1,0:T(8,128)} %conn_hbm.3) | copy-start | bytes 294916
  46.2 1.4 %copy-start = (f32[3072,128]{1,0:T(8,128)S(1)}, f32[3072,128]{1,0:T(8,128)}, u32[]{:S(2)}) copy-start(f32[3072,128]{1,0:T(8,128)} %forward.1.con_ref) | copy-start | bytes 4718596
  57.2 18.0 %copy-start.2 = (s32[2,1024]{1,0:T(2,128)S(1)}, s32[2,1024]{1,0:T(2,128)}, u32[]{:S(2)}) copy-start(s32[2,1024]{1,0:T(2,128)} %faces_hbm.3) | copy-start | bytes 24580

commit v3 on v2

--- a/solution.py
+++ b/solution.py
@@ -31,12 +31,28 @@
     weight = np.where((c == 0) | (c == 63), 1.0 / length, 2.0 / length)
     inverse = np.kron(np.eye(2), basis)
     forward = np.kron(np.eye(2), (basis * weight[:, None]).T)
-    return inverse.astype(np.float32), forward.astype(np.float32)
+    return split_table(inverse), split_table(forward)
+
+
+def split_table(table):
+    high = table.astype(jnp.bfloat16)
+    rest = (table - high.astype(np.float64)).astype(jnp.bfloat16)
+    return np.block([[high, rest], [high, np.zeros_like(rest)]])
+
+
+def transform(parts, table_ref):
+    x = jnp.concatenate(parts, axis=0)
+    high = x.astype(jnp.bfloat16)
+    rest = (x - high.astype(jnp.float32)).astype(jnp.bfloat16)
+    y = jnp.dot(jnp.concatenate([high, rest], axis=1), table_ref[...], preferred_element_type=jnp.float32)
+    y = y[:, 0:128] + y[:, 128:256]
+    n = parts[0].shape[0]
+    return [y[i * n:(i + 1) * n, :] for i in range(len(parts))]
 
 
 def forward_kernel(field_ref, point_ref, mat_ref, curl_ref, faces_hbm, conn_hbm, knots_ref, base_ref, slopes_ref,
-                   inv_ref, fwd_ref, out_ref,
-                   field, point, curl, opsend, op_in, field_t, face_rows, face_cols, ext, ext2, curl_t, wide, got, flux, faces_ref, conn_ref,
+                   inv_hbm, fwd_hbm, out_ref,
+                   field, point, curl, opsend, op_in, field_t, face_rows, face_cols, ext, ext2, curl_t, wide, got, flux, inv_ref, fwd_ref, faces_ref, conn_ref,
                    in_s, op_ss, op_rs, far_ss, far_rs, side_ss, side_rs, gh_ss, gh_rs, fw_ss, fw_rs, rel_ss, rel_rs, idx_s):
     m = lax.axis_index("mesh")
     h = lax.axis_index("harm")
@@ -59,6 +75,8 @@
                   for f in range(2)]
     load_conn = [pltpu.make_async_copy(conn_hbm.at[j], conn_ref.at[pl.ds(j * 4096, 4096)], idx_s.at[2 + j])
                  for j in range(6)]
+    load_conn.append(pltpu.make_async_copy(inv_hbm, inv_ref, idx_s.at[8]))
+    load_conn.append(pltpu.make_async_copy(fwd_hbm, fwd_ref, idx_s.at[9]))
     for c in (*load_faces, *load_conn):
         c.start()
 
@@ -137,17 +155,20 @@
         opsend[p, pl.ds(48, 8), :] = jnp.zeros((8, 128), jnp.float32)
         opsend[p, pl.ds(48, 1), pl.ds(0, 32)] = mat_ref[pl.ds(p, 1), :].astype(jnp.float32)
 
-    def op_copy(d):
-        p = lax.rem(m + d, N_MESH)
-        target = lax.rem(h + 2 * ((half + p // 16) % 2) * lax.rem(m, 2), 4)
+    within = lax.rem(m, 16)
+
+    def op_copy(slot):
+        cross = slot // 16
+        p = lax.rem(half + cross, 2) * 16 + lax.rem(within + slot, 16)
+        target = lax.rem(h + 2 * cross * lax.rem(m, 2), 4)
         return pltpu.make_async_remote_copy(
             src_ref=opsend.at[p], dst_ref=op_in.at[m],
-            send_sem=op_ss.at[d], recv_sem=op_rs.at[d],
+            send_sem=op_ss.at[slot], recv_sem=op_rs.at[slot],
             device_id=(p, target), device_id_type=MESH)
 
-    @pl.loop(1, N_MESH)
-    def _(d):
-        op_copy(d).start()
+    @pl.loop(1, 16)
+    def _(slot):
+        op_copy(slot).start()
     op_keep = pltpu.make_async_copy(opsend.at[m], op_in.at[m], in_s.at[4])
     op_keep.start()
 
@@ -203,6 +224,11 @@
     gfar.wait_recv()
     relays[PARTS].start()
 
+    @pl.loop(16, N_MESH)
+    def _(slot):
+        op_copy(slot).start()
+
+
     for c in load_conn:
         c.wait()
     keep.wait()
@@ -220,25 +246,27 @@
             x = ext[:, at]
             ext2[at, :] = jnp.concatenate([x, x], axis=0).T
 
-    @pl.loop(0, N_MESH)
-    def _(s):
-        to = pl.ds(pl.multiple_of(s * 16, 16), 16)
-        first = pl.multiple_of(s * 128 + block_of(s, m) * 32, 32)
-        near = conn_ref.at[pl.ds(first, 5 * 4096 + 32)]
-        for j in range(6):
-            for k in range(16):
-                a = ext2[pl.ds(near[j * 4096 + k], 1), :]
-                b = ext2[pl.ds(near[j * 4096 + 16 + k], 1), :]
-                got[pl.ds(j * 16 + k, 1), :] = jnp.where(low1, a, b)
-        for i in range(3):
-            s_i = wide[i * 6, to, :] * got[0:16, :]
-            for j in range(1, 6):
-                s_i = s_i + wide[i * 6 + j, to, :] * got[j * 16:(j + 1) * 16, :]
-            flux[i, to, :] = s_i
+    @pl.loop(0, N_MESH // 2)
+    def _(pair):
+        for u in range(2):
+            s = pair * 2 + u
+            to = pl.ds(pl.multiple_of(s * 16, 16), 16)
+            first = pl.multiple_of(s * 128 + block_of(s, m) * 32, 32)
+            near = conn_ref.at[pl.ds(first, 5 * 4096 + 32)]
+            for j in range(6):
+                for k in range(16):
+                    a = ext2[pl.ds(near[j * 4096 + k], 1), :]
+                    b = ext2[pl.ds(near[j * 4096 + 16 + k], 1), :]
+                    got[u, pl.ds(j * 16 + k, 1), :] = jnp.where(low1, a, b)
+            for i in range(3):
+                s_i = wide[i * 6, to, :] * got[u, 0:16, :]
+                for j in range(1, 6):
+                    s_i = s_i + wide[i * 6 + j, to, :] * got[u, j * 16:(j + 1) * 16, :]
+                flux[i, to, :] = s_i
 
     @pl.loop(1, N_MESH)
-    def _(d):
-        op_copy(d).wait_recv()
+    def _(slot):
+        op_copy(slot).wait_recv()
 
     op_keep.wait()
     growth = [jnp.exp(jnp.float32(-0.5) * knots_ref[k].astype(jnp.float32)) for k in range(8)]
@@ -246,8 +274,7 @@
     @pl.loop(0, ROWS // 64)
     def _(r):
         to = pl.ds(pl.multiple_of(r * 64, 64), 64)
-        f = [jnp.dot(flux[i, to, :], inv_ref[...], precision=lax.Precision.HIGHEST,
-                     preferred_element_type=jnp.float32) for i in range(3)]
+        f = transform([flux[i, to, :] for i in range(3)], inv_ref)
         b = [jnp.concatenate([op_in[r * 4 + s, 16 * i:16 * i + 16, :] for s in range(4)], axis=0)
              for i in range(3)]
         kinds = []
@@ -266,61 +293,61 @@
         u = jnp.exp(2.0 * q)
         nu = pick([base_ref[a] for a in range(4)])
         dnu = jnp.zeros_like(q)
-        for k in range(8):
-            slope = pick([slopes_ref[a, k] for a in range(4)])
-            e = u * growth[k]
-            w = 1.0 + e
-            nu = nu + slope * jnp.log(w)
-            dnu = dnu + slope * (e / w)
+        for k in range(0, 8, 2):
+            s0, s1 = [pick([slopes_ref[a, k + n] for a in range(4)]) for n in range(2)]
+            e0, e1 = u * growth[k], u * growth[k + 1]
+            w0, w1 = 1.0 + e0, 1.0 + e1
+            nu = nu + s0 * jnp.log(w0) + s1 * jnp.log(w1)
+            dnu = dnu + (s0 * e0 * w1 + s1 * e1 * w0) / (w0 * w1)
         proj = b[0] * f[0] + b[1] * f[1] + b[2] * f[2]
         scale = 4.0 * dnu * proj
-        f = [jnp.dot(nu * f[i] + scale * b[i], fwd_ref[...], precision=lax.Precision.HIGHEST,
-                     preferred_element_type=jnp.float32) for i in range(3)]
+        f = transform([nu * f[i] + scale * b[i] for i in range(3)], fwd_ref)
         for j in range(6):
-            out_ref[pl.ds(pl.multiple_of(j * ROWS + r * 64, 64), 64), :] = (
+            out_ref[r, j * 64:(j + 1) * 64, :] = (
                 wide[j, to, :] * f[0] + wide[6 + j, to, :] * f[1] + wide[12 + j, to, :] * f[2])
 
     for c in (*to_far, *to_side, *ghosts, gfar, gside, *relays):
         c.wait_send()
 
     @pl.loop(1, N_MESH)
-    def _(d):
-        op_copy(d).wait_send()
+    def _(slot):
+        op_copy(slot).wait_send()
 
 
 def forward(field, point, material, curl, faces, conn, knots, base, slopes):
     inverse, forward_table = block_diag_tables()
     smem = pl.BlockSpec(memory_space=pltpu.SMEM)
     vmem = pl.BlockSpec(memory_space=pltpu.VMEM)
-    hbm = pl.BlockSpec(memory_space=pl.ANY)
+    hbm = pl.BlockSpec(memory_space=pltpu.HBM)
     f32 = jnp.float32
     dma = pltpu.SemaphoreType.DMA
     return pl.pallas_call(
         forward_kernel,
         name="forward",
-        out_shape=jax.ShapeDtypeStruct((6 * ROWS, 128), f32),
-        in_specs=[hbm, hbm, vmem, hbm, hbm, hbm, smem, smem, smem, vmem, vmem],
+        out_shape=jax.ShapeDtypeStruct((ROWS // 64, 384, 128), f32),
+        in_specs=[hbm, hbm, vmem, hbm, hbm, hbm, smem, smem, smem, hbm, hbm],
         out_specs=vmem,
         scratch_shapes=[
             pltpu.VMEM((16, OWN), f32), pltpu.VMEM((3, 32, 32, 64), f32), pltpu.VMEM((3, 6, 4096), f32),
             pltpu.VMEM((N_MESH, MSG, 128), f32), pltpu.VMEM((N_MESH, MSG, 128), f32),
             pltpu.VMEM((OWN, 16), f32), pltpu.VMEM((2 * FACE, 16), f32), pltpu.VMEM((16, 2 * FACE), f32),
             pltpu.VMEM((64, EXT), f32), pltpu.VMEM((EXT, 128), f32), pltpu.VMEM((4096, 24), f32),
-            pltpu.VMEM((18, ROWS, 128), f32), pltpu.VMEM((96, 128), f32), pltpu.VMEM((3, ROWS, 128), f32),
+            pltpu.VMEM((18, ROWS, 128), f32), pltpu.VMEM((2, 96, 128), f32), pltpu.VMEM((3, ROWS, 128), f32),
+            pltpu.VMEM((256, 256), jnp.bfloat16), pltpu.VMEM((256, 256), jnp.bfloat16),
             pltpu.SMEM((2 * FACE,), jnp.int32), pltpu.SMEM((6 * 4096,), jnp.int32),
             dma((5,)), dma((N_MESH,)), dma((N_MESH,)), dma((PARTS,)), dma((PARTS,)), dma((PARTS,)), dma((PARTS,)),
-            dma((2,)), dma((2,)), dma((2,)), dma((2,)), dma((PARTS + 1,)), dma((PARTS + 1,)), dma((8,)),
+            dma((2,)), dma((2,)), dma((2,)), dma((2,)), dma((PARTS + 1,)), dma((PARTS + 1,)), dma((10,)),
         ],
         compiler_params=pltpu.CompilerParams(collective_id=0, has_side_effects=True,
-                                             vmem_limit_bytes=60 << 20),
-    )(field, point, material, curl, faces, conn, knots, base, slopes, jnp.asarray(inverse), jnp.asarray(forward_table))
-
-
-def scatter_kernel(conn_hbm, con_ref, out_ref, acc0, acc1, acc2, acc3, acc4, acc5, conn_ref, sem):
+                                             vmem_limit_bytes=34 << 20),
+    )(field, point, material, curl, faces, conn, knots, base, slopes, pltpu.with_memory_space_constraint(jnp.asarray(inverse), pltpu.HBM),
+      pltpu.with_memory_space_constraint(jnp.asarray(forward_table), pltpu.HBM))
+
+
+def scatter_kernel(conn_hbm, con_ref, acc0, acc1, acc2, acc3, acc4, acc5, conn_ref, sem):
     m = lax.axis_index("mesh")
     h = lax.axis_index("harm")
     accs = (acc0, acc1, acc2, acc3, acc4, acc5)
-    low = lax.broadcasted_iota(jnp.int32, (64, 128), 1) < 64
 
     def block_of(source, target):
         crossing = (source // 16 + target // 16) % 2
@@ -343,36 +370,31 @@
     def _(s):
         first = pl.multiple_of(s * 128 + block_of(s, m) * 32, 32)
         near = conn_ref.at[pl.ds(first, 5 * 4096 + 32)]
+        rows = con_ref.at[s // 4, pl.ds(pl.multiple_of(lax.rem(s, 4) * 16, 16), 336), :]
         for k in range(16):
             for j in range(6):
-                row = con_ref[pl.ds(j * ROWS + s * 16 + k, 1), :]
+                row = rows[pl.ds(j * 64 + k, 1), :]
                 n0 = near[j * 4096 + k]
                 n1 = near[j * 4096 + 16 + k]
                 a0, a1 = accs[j % 3], accs[3 + j % 3]
                 a0[pl.ds(n0, 1), :] = a0[pl.ds(n0, 1), :] + row
                 a1[pl.ds(n1, 1), :] = a1[pl.ds(n1, 1), :] + row
 
-    @pl.loop(0, EXT // 64, unroll=2)
-    def _(b):
-        at = pl.ds(pl.multiple_of(b * 64, 64), 64)
-        out_ref[at, :] = jnp.where(low, acc0[at, :] + acc1[at, :] + acc2[at, :], acc3[at, :] + acc4[at, :] + acc5[at, :])
-
 
 def scatter(conn, con):
     vmem = pl.BlockSpec(memory_space=pltpu.VMEM)
-    big = pltpu.VMEM((EXT, 128), jnp.float32)
     return pl.pallas_call(
         scatter_kernel,
         name="scatter",
-        out_shape=jax.ShapeDtypeStruct((EXT, 128), jnp.float32),
-        in_specs=[pl.BlockSpec(memory_space=pl.ANY), vmem],
-        out_specs=vmem,
-        scratch_shapes=[big, big, big, big, big, big, pltpu.SMEM((6 * 4096,), jnp.int32), pltpu.SemaphoreType.DMA((6,))],
-        compiler_params=pltpu.CompilerParams(vmem_limit_bytes=32 << 20),
+        out_shape=(jax.ShapeDtypeStruct((EXT, 128), jnp.float32),) * 6,
+        in_specs=[pl.BlockSpec(memory_space=pltpu.HBM), vmem],
+        out_specs=(vmem,) * 6,
+        scratch_shapes=[pltpu.SMEM((6 * 4096,), jnp.int32), pltpu.SemaphoreType.DMA((6,))],
+        compiler_params=pltpu.CompilerParams(vmem_limit_bytes=28 << 20),
     )(conn, con)
 
 
-def combine_kernel(rows_ref, own_out, ghost_out, acc, pairs, summed, zin, ghost_sum, ghost_in,
+def combine_kernel(acc0, acc1, acc2, acc3, acc4, acc5, own_out, ghost_out, acc, pairs, summed, zin, ghost_sum, ghost_in,
                    p_ss, p_rs, z_ss, z_rs, g_ss, g_rs):
     m = lax.axis_index("mesh")
     h = lax.axis_index("harm")
@@ -384,11 +406,13 @@
     for peer in ((m, side), (m, far), (up, h), (down, h)):
         pl.semaphore_signal(barrier, inc=1, device_id=peer, device_id_type=MESH)
 
-    bounds = [(OWN, 2 * FACE)] + [(c * CHUNK, CHUNK) for c in range(PARTS)]
+    bounds = [(OWN, FACE), (OWN + FACE, FACE)] + [(c * CHUNK, CHUNK) for c in range(PARTS)]
     chunks = [pl.ds(a, n) for a, n in bounds]
 
     def block(who):
         return pl.ds(pl.multiple_of(16 * who, 16), 16)
+
+    low = lax.broadcasted_iota(jnp.int32, (128, 128), 1) < 64
 
     def turn(c):
         start, n = bounds[c]
@@ -396,7 +420,7 @@
         @pl.loop(0, n // 128, unroll=2)
         def _(b):
             at = pl.ds(pl.multiple_of(start + b * 128, 128), 128)
-            x = rows_ref[at, :].T
+            x = jnp.where(low, acc0[at, :] + acc1[at, :] + acc2[at, :], acc3[at, :] + acc4[at, :] + acc5[at, :]).T
             acc[:, at] = x[0:64, :] + x[64:128, :]
 
     def pair_copy(c, n):
@@ -418,7 +442,7 @@
             send_sem=g_ss.at[f], recv_sem=g_rs.at[f],
             device_id=(peer, h), device_id_type=MESH)
 
-    count = PARTS + 1
+    count = PARTS + 2
     far_pairs = [pair_copy(c, 1) for c in range(count)]
     own_pairs = [pair_copy(c, 0) for c in range(count)]
     zs = [z_copy(c) for c in range(count)]
@@ -442,10 +466,10 @@
         zs[c].wait_recv()
         return acc[block(h), chunks[c]] + pairs[0, :, chunks[c]] + zin[:, chunks[c]]
 
-    ghost_sum[...] = total(0)
-    for g in gs:
-        g.start()
-    for c in range(1, count):
+    for f in range(2):
+        ghost_sum[:, pl.ds(f * FACE, FACE)] = total(f)
+        gs[f].start()
+    for c in range(2, count):
         own_out[:, chunks[c]] = total(c)
     for g in gs:
         g.wait_recv()
@@ -454,7 +478,7 @@
         c.wait_send()
 
 
-def combine(rows):
+def combine(accs):
     vmem = pl.BlockSpec(memory_space=pltpu.VMEM)
     dma = pltpu.SemaphoreType.DMA
     f32 = jnp.float32
@@ -462,16 +486,16 @@
         combine_kernel,
         name="combine",
         out_shape=(jax.ShapeDtypeStruct((16, OWN), f32), jax.ShapeDtypeStruct((16, 2 * FACE), f32)),
-        in_specs=[vmem],
+        in_specs=[vmem] * 6,
         out_specs=(vmem, vmem),
         scratch_shapes=[
             pltpu.VMEM((64, EXT), f32), pltpu.VMEM((2, 16, EXT), f32), pltpu.VMEM((16, EXT), f32),
             pltpu.VMEM((16, EXT), f32), pltpu.VMEM((16, 2 * FACE), f32), pltpu.VMEM((16, 2 * FACE), f32),
-            dma((PARTS + 1, 2)), dma((PARTS + 1, 2)), dma((PARTS + 1,)), dma((PARTS + 1,)), dma((2,)), dma((2,)),
+            dma((PARTS + 2, 2)), dma((PARTS + 2, 2)), dma((PARTS + 2,)), dma((PARTS + 2,)), dma((2,)), dma((2,)),
         ],
         compiler_params=pltpu.CompilerParams(collective_id=1, has_side_effects=True,
-                                             vmem_limit_bytes=32 << 20),
-    )(rows)
+                                             vmem_limit_bytes=28 << 20),
+    )(*accs)
 
 
 def finish_kernel(faces_hbm, own_ref, ghost_ref, out_ref, ghost_t, full_t, faces_ref, idx_s):
@@ -522,6 +546,9 @@
 def per_device(field_in, faces, connectivity, curl_vectors, operating_point, material, bh_knots, curve_base,
                curve_slopes):
     point = jnp.transpose(operating_point, (1, 2, 3, 0))
+    (field_in, point, material, curl_vectors, faces, connectivity, bh_knots, curve_base, curve_slopes) = [
+        pltpu.with_memory_space_constraint(x, pltpu.HBM)
+        for x in (field_in, point, material, curl_vectors, faces, connectivity, bh_knots, curve_base, curve_slopes)]
     contributions = forward(field_in, point, material, curl_vectors, faces, connectivity, bh_knots, curve_base,
                             curve_slopes)
     own, ghost = combine(scatter(connectivity, contributions))

time: 79.6 us -> 72.6 us (0.912)
  Pallas kernels: 78 us -> 72.2 us
  local copies, waits for them, and re-layouts: 1.41 us -> 0 us
    pallas_call x1, Pallas kernels: 46.1 us -> 37.7 us  [forward(): pl.pallas_call(forward_kernel, name='forward', out_shape=jax.ShapeDtypeSt...]
    pallas_call x1, Pallas kernels: 18 us -> 21.5 us  [combine(): pl.pallas_call(combine_kernel, name='combine', out_shape=(jax.ShapeDtypeS...]
    unnamed x6 -> x0, local copies, waits for them, and re-layouts: 1.41 us -> none
    pallas_call x1, Pallas kernels: 9.59 us -> 8.61 us  [scatter(): pl.pallas_call(scatter_kernel, name='scatter', out_shape=(jax.ShapeDtypeS...]
where the time goes in v3:
time: 72.6 us; the launch traced here: 72.2 us
  Pallas kernels  72.2 us (99%)
    pallas_call x1, Pallas kernels, forward(): pl.pallas_call(forward_kernel, name='forward', out_shape=jax.ShapeDtypeSt...  37.7 us
    pallas_call x1, Pallas kernels, combine(): pl.pallas_call(combine_kernel, name='combine', out_shape=(jax.ShapeDtypeS...  21.5 us
    pallas_call x1, Pallas kernels, scatter(): pl.pallas_call(scatter_kernel, name='scatter', out_shape=(jax.ShapeDtypeS...  8.61 us
    pallas_call x1, Pallas kernels, finish(): pl.pallas_call(finish_kernel, name='finish', out_shape=jax.ShapeDtypeStru...  4.39 us

profile of v3, /device:TPU:1, one launch (start us, length us, event | category | flops | bytes accessed | tf_op | source)
XLA Modules:
  0.0 72.2 jit_solution(10441590379363584522)
XLA Ops:
  0.0 37.7 %forward.1.con_ref = f32[8,384,128]{2,1,0:T(8,128)S(1)} custom-call(f32[16,5120]{1,0:T(8,128)} %field_ref.1, f32[3,32,32,64]{3,2,1,0:T(8,128)} %bitcast.1, s32[32,32]{1,0:T(8,128)} %mat_ref.1, f32[3,6,4096]{2,1,0:T(8,128)} %curl_ref.1, s32[2,1024]{1,0:T(2,128)} %faces_hbm.3, s32[6,4096]{1,0:T(8,128)} %conn_hbm.3, s32[8]{0:T(128)} %knots_ref.1, f32[4]{0:T(128)} %base_ref.1, ...), custom_call_target="tpu_custom_call" | custom-call | tf_op jit(solution)/shard_map/forward/pallas_call | solution.py:324
  37.7 8.6 %scatter.1 = (f32[7168,128]{1,0:T(8,128)S(1)}, f32[7168,128]{1,0:T(8,128)S(1)}, f32[7168,128]{1,0:T(8,128)S(1)}, f32[7168,128]{1,0:T(8,128)S(1)}, f32[7168,128]{1,0:T(8,128)S(1)}, /*index=5*/f32[7168,128]{1,0:T(8,128)S(1)}) custom-call(s32[6,4096]{1,0:T(8,128)} %conn_hbm.3, f32[8,384,128]{2,1,0:T(8,128)S(1)} %forward.1.con_ref), custom_call_target="tpu_custom_call" | custom-call | tf_op jit(solution)/shard_map/scatter/pallas_call | solution.py:386
  46.3 21.5 %combine.1 = (f32[16,5120]{1,0:T(8,128)S(1)}, f32[16,2048]{1,0:T(8,128)S(1)}) custom-call(f32[7168,128]{1,0:T(8,128)S(1)} %get-tuple-element.13.acc0, f32[7168,128]{1,0:T(8,128)S(1)} %get-tuple-element.14.acc1, f32[7168,128]{1,0:T(8,128)S(1)} %get-tuple-element.15.acc2, f32[7168,128]{1,0:T(8,128)S(1)} %get-tuple-element.16.acc3, ...), custom_call_target="tpu_custom_call" | custom-call | tf_op jit(solution)/shard_map/combine/pallas_call | solution.py:485
  67.8 4.4 %finish.1 = f32[16,5120]{1,0:T(8,128)} custom-call(s32[2,1024]{1,0:T(2,128)} %faces_hbm.3, f32[16,5120]{1,0:T(8,128)S(1)} %get-tuple-element.19.own_ref, f32[16,2048]{1,0:T(8,128)S(1)} %get-tuple-element.20.ghost_ref), custom_call_target="tpu_custom_call" | custom-call | tf_op jit(solution)/shard_map/finish/pallas_call | solution.py:534

commit v4 on v3

--- a/solution.py
+++ b/solution.py
@@ -17,6 +17,7 @@
 MSG = 56
 PARTS = 4
 CHUNK = OWN // PARTS
+EDGE_ORDER = [(j + 3 * g, k) for g in range(2) for k in range(16) for j in range(3)]
 
 
 def block_diag_tables():
@@ -64,6 +65,23 @@
     def block_of(source, target):
         crossing = (source // 16 + target // 16) % 2
         return lax.rem(h + 2 * crossing * lax.rem(source, 2), 4)
+
+    within = lax.rem(m, 16)
+    barrier = pltpu.get_barrier_semaphore()
+    crossing_h = [h, far]
+    for peer in ((m, far), (m, side), (up, h), (down, h)):
+        pl.semaphore_signal(barrier, inc=1, device_id=peer, device_id_type=MESH)
+
+    @pl.loop(1, 16, unroll=3)
+    def _(d):
+        other = lax.rem(within + d, 16)
+        pl.semaphore_signal(barrier, inc=1, device_id=(half * 16 + other, h), device_id_type=MESH)
+
+    for odd in range(2):
+        @pl.loop(0, 8, unroll=2)
+        def _(d):
+            pl.semaphore_signal(barrier, inc=1, device_id=((1 - half) * 16 + 2 * d + odd, crossing_h[odd]),
+                                device_id_type=MESH)
 
     load_field = pltpu.make_async_copy(field_ref, field, in_s.at[0])
     load_point = pltpu.make_async_copy(point_ref, point, in_s.at[1])
@@ -80,21 +98,7 @@
     for c in (*load_faces, *load_conn):
         c.start()
 
-    barrier = pltpu.get_barrier_semaphore()
-    for peer in ((m, far), (m, side), (up, h), (down, h)):
-        pl.semaphore_signal(barrier, inc=1, device_id=peer, device_id_type=MESH)
-
-    @pl.loop(1, N_MESH)
-    def _(d):
-        source = lax.rem(m + N_MESH - d, N_MESH)
-        pl.semaphore_signal(barrier, inc=1, device_id=(source, block_of(source, m)), device_id_type=MESH)
-
     load_field.wait()
-
-    @pl.loop(0, OWN // 128, unroll=8)
-    def _(b):
-        at = pl.ds(pl.multiple_of(b * 128, 128), 128)
-        field_t[at, :] = field[:, at].T
 
     pl.semaphore_wait(barrier, N_MESH - 1 + 4)
 
@@ -118,6 +122,11 @@
         c.start()
     keep = pltpu.make_async_copy(field, ext.at[rows_of(h), pl.ds(0, OWN)], in_s.at[3])
     keep.start()
+
+    @pl.loop(0, OWN // 128, unroll=8)
+    def _(b):
+        at = pl.ds(pl.multiple_of(b * 128, 128), 128)
+        field_t[at, :] = field[:, at].T
 
     for c in load_faces:
         c.wait()
@@ -155,15 +164,13 @@
         opsend[p, pl.ds(48, 8), :] = jnp.zeros((8, 128), jnp.float32)
         opsend[p, pl.ds(48, 1), pl.ds(0, 32)] = mat_ref[pl.ds(p, 1), :].astype(jnp.float32)
 
-    within = lax.rem(m, 16)
-
     def op_copy(slot):
         cross = slot // 16
         p = lax.rem(half + cross, 2) * 16 + lax.rem(within + slot, 16)
         target = lax.rem(h + 2 * cross * lax.rem(m, 2), 4)
         return pltpu.make_async_remote_copy(
             src_ref=opsend.at[p], dst_ref=op_in.at[m],
-            send_sem=op_ss.at[slot], recv_sem=op_rs.at[slot],
+            send_sem=op_ss, recv_sem=op_rs,
             device_id=(p, target), device_id_type=MESH)
 
     @pl.loop(1, 16)
@@ -221,12 +228,15 @@
                                                        jnp.broadcast_to(c1[:, col:col + 1], (16, 128)))
         to_far[c].wait_recv()
         relays[c].start()
+        if c == PARTS - 2:
+            @pl.loop(16, N_MESH)
+            def _(slot):
+                op_copy(slot).start()
     gfar.wait_recv()
     relays[PARTS].start()
 
-    @pl.loop(16, N_MESH)
-    def _(slot):
-        op_copy(slot).start()
+    for c in (*to_far, *to_side, *ghosts, gfar, gside):
+        c.wait_send()
 
 
     for c in load_conn:
@@ -252,21 +262,21 @@
             s = pair * 2 + u
             to = pl.ds(pl.multiple_of(s * 16, 16), 16)
             first = pl.multiple_of(s * 128 + block_of(s, m) * 32, 32)
-            near = conn_ref.at[pl.ds(first, 5 * 4096 + 32)]
-            for j in range(6):
-                for k in range(16):
-                    a = ext2[pl.ds(near[j * 4096 + k], 1), :]
-                    b = ext2[pl.ds(near[j * 4096 + 16 + k], 1), :]
-                    got[u, pl.ds(j * 16 + k, 1), :] = jnp.where(low1, a, b)
+            near = [conn_ref.at[pl.ds(first + j * 4096, 32)] for j in range(6)]
+            for j, k in EDGE_ORDER:
+                a = ext2[pl.ds(near[j][k], 1), :]
+                b = ext2[pl.ds(near[j][16 + k], 1), :]
+                got[u, pl.ds(j * 16 + k, 1), :] = jnp.where(low1, a, b)
             for i in range(3):
                 s_i = wide[i * 6, to, :] * got[u, 0:16, :]
                 for j in range(1, 6):
                     s_i = s_i + wide[i * 6 + j, to, :] * got[u, j * 16:(j + 1) * 16, :]
                 flux[i, to, :] = s_i
 
-    @pl.loop(1, N_MESH)
-    def _(slot):
-        op_copy(slot).wait_recv()
+    op_all = pltpu.make_async_remote_copy(
+        src_ref=opsend.at[pl.ds(0, N_MESH - 1)], dst_ref=op_in.at[pl.ds(0, N_MESH - 1)],
+        send_sem=op_ss, recv_sem=op_rs, device_id=(m, far), device_id_type=MESH)
+    op_all.wait_recv()
 
     op_keep.wait()
     growth = [jnp.exp(jnp.float32(-0.5) * knots_ref[k].astype(jnp.float32)) for k in range(8)]
@@ -306,12 +316,10 @@
             out_ref[r, j * 64:(j + 1) * 64, :] = (
                 wide[j, to, :] * f[0] + wide[6 + j, to, :] * f[1] + wide[12 + j, to, :] * f[2])
 
-    for c in (*to_far, *to_side, *ghosts, gfar, gside, *relays):
+    for c in relays:
         c.wait_send()
 
-    @pl.loop(1, N_MESH)
-    def _(slot):
-        op_copy(slot).wait_send()
+    op_all.wait_send()
 
 
 def forward(field, point, material, curl, faces, conn, knots, base, slopes):
@@ -335,7 +343,7 @@
             pltpu.VMEM((18, ROWS, 128), f32), pltpu.VMEM((2, 96, 128), f32), pltpu.VMEM((3, ROWS, 128), f32),
             pltpu.VMEM((256, 256), jnp.bfloat16), pltpu.VMEM((256, 256), jnp.bfloat16),
             pltpu.SMEM((2 * FACE,), jnp.int32), pltpu.SMEM((6 * 4096,), jnp.int32),
-            dma((5,)), dma((N_MESH,)), dma((N_MESH,)), dma((PARTS,)), dma((PARTS,)), dma((PARTS,)), dma((PARTS,)),
+            dma((5,)), dma, dma, dma((PARTS,)), dma((PARTS,)), dma((PARTS,)), dma((PARTS,)),
             dma((2,)), dma((2,)), dma((2,)), dma((2,)), dma((PARTS + 1,)), dma((PARTS + 1,)), dma((10,)),
         ],
         compiler_params=pltpu.CompilerParams(collective_id=0, has_side_effects=True,
@@ -369,16 +377,15 @@
     @pl.loop(0, N_MESH)
     def _(s):
         first = pl.multiple_of(s * 128 + block_of(s, m) * 32, 32)
-        near = conn_ref.at[pl.ds(first, 5 * 4096 + 32)]
+        near = [conn_ref.at[pl.ds(first + j * 4096, 32)] for j in range(6)]
         rows = con_ref.at[s // 4, pl.ds(pl.multiple_of(lax.rem(s, 4) * 16, 16), 336), :]
-        for k in range(16):
-            for j in range(6):
-                row = rows[pl.ds(j * 64 + k, 1), :]
-                n0 = near[j * 4096 + k]
-                n1 = near[j * 4096 + 16 + k]
-                a0, a1 = accs[j % 3], accs[3 + j % 3]
-                a0[pl.ds(n0, 1), :] = a0[pl.ds(n0, 1), :] + row
-                a1[pl.ds(n1, 1), :] = a1[pl.ds(n1, 1), :] + row
+        for j, k in EDGE_ORDER:
+            row = rows[pl.ds(j * 64 + k, 1), :]
+            n0 = near[j][k]
+            n1 = near[j][16 + k]
+            a0, a1 = accs[j % 3], accs[3 + j % 3]
+            a0[pl.ds(n0, 1), :] = a0[pl.ds(n0, 1), :] + row
+            a1[pl.ds(n1, 1), :] = a1[pl.ds(n1, 1), :] + row
 
 
 def scatter(conn, con):
@@ -518,10 +525,11 @@
 
     @pl.loop(0, 2 * FACE // 32)
     def _(b):
-        near = faces_ref.at[pl.ds(pl.multiple_of(b * 32, 32), 32)]
         rows = ghost_t.at[pl.ds(pl.multiple_of(b * 32, 32), 32), :]
-        for k in range(32):
-            full_t[pl.ds(near[k], 1), :] = rows[pl.ds(k, 1), :]
+        for g in range(4):
+            near = faces_ref.at[pl.ds(pl.multiple_of(b * 32 + g * 8, 8), 8)]
+            for k in range(8):
+                full_t[pl.ds(near[k], 1), :] = rows[pl.ds(g * 8 + k, 1), :]
 
     @pl.loop(0, OWN // 128, unroll=8)
     def _(b):

time: 72.6 us -> 70.1 us (0.966)
  Pallas kernels: 72.2 us -> 69.7 us
    pallas_call x1, Pallas kernels: 37.7 us -> 36.4 us  [forward(): pl.pallas_call(forward_kernel, name='forward', out_shape=jax.ShapeDtypeSt...]
where the time goes in v4:
time: 70.1 us; the launch traced here: 69.8 us
  Pallas kernels  69.7 us (99%)
    pallas_call x1, Pallas kernels, forward(): pl.pallas_call(forward_kernel, name='forward', out_shape=jax.ShapeDtypeSt...  36.4 us
    pallas_call x1, Pallas kernels, combine(): pl.pallas_call(combine_kernel, name='combine', out_shape=(jax.ShapeDtypeS...  20.8 us
    pallas_call x1, Pallas kernels, scatter(): pl.pallas_call(scatter_kernel, name='scatter', out_shape=(jax.ShapeDtypeS...  8.51 us
    pallas_call x1, Pallas kernels, finish(): pl.pallas_call(finish_kernel, name='finish', out_shape=jax.ShapeDtypeStru...  4.02 us

profile of v4, /device:TPU:1, one launch (start us, length us, event | category | flops | bytes accessed | tf_op | source)
XLA Modules:
  0.0 69.8 jit_solution(2360292185864580995)
XLA Ops:
  0.0 36.4 %forward.1.con_ref = f32[8,384,128]{2,1,0:T(8,128)S(1)} custom-call(f32[16,5120]{1,0:T(8,128)} %field_ref.1, f32[3,32,32,64]{3,2,1,0:T(8,128)} %bitcast.1, s32[32,32]{1,0:T(8,128)} %mat_ref.1, f32[3,6,4096]{2,1,0:T(8,128)} %curl_ref.1, s32[2,1024]{1,0:T(2,128)} %faces_hbm.3, s32[6,4096]{1,0:T(8,128)} %conn_hbm.3, s32[8]{0:T(128)} %knots_ref.1, f32[4]{0:T(128)} %base_ref.1, ...), custom_call_target="tpu_custom_call" | custom-call | tf_op jit(solution)/shard_map/forward/pallas_call | solution.py:332
  36.4 8.5 %scatter.1 = (f32[7168,128]{1,0:T(8,128)S(1)}, f32[7168,128]{1,0:T(8,128)S(1)}, f32[7168,128]{1,0:T(8,128)S(1)}, f32[7168,128]{1,0:T(8,128)S(1)}, f32[7168,128]{1,0:T(8,128)S(1)}, /*index=5*/f32[7168,128]{1,0:T(8,128)S(1)}) custom-call(s32[6,4096]{1,0:T(8,128)} %conn_hbm.3, f32[8,384,128]{2,1,0:T(8,128)S(1)} %forward.1.con_ref), custom_call_target="tpu_custom_call" | custom-call | tf_op jit(solution)/shard_map/scatter/pallas_call | solution.py:393
  44.9 20.8 %combine.1 = (f32[16,5120]{1,0:T(8,128)S(1)}, f32[16,2048]{1,0:T(8,128)S(1)}) custom-call(f32[7168,128]{1,0:T(8,128)S(1)} %get-tuple-element.13.acc0, f32[7168,128]{1,0:T(8,128)S(1)} %get-tuple-element.14.acc1, f32[7168,128]{1,0:T(8,128)S(1)} %get-tuple-element.15.acc2, f32[7168,128]{1,0:T(8,128)S(1)} %get-tuple-element.16.acc3, ...), custom_call_target="tpu_custom_call" | custom-call | tf_op jit(solution)/shard_map/combine/pallas_call | solution.py:492
  65.7 4.0 %finish.1 = f32[16,5120]{1,0:T(8,128)} custom-call(s32[2,1024]{1,0:T(2,128)} %faces_hbm.3, f32[16,5120]{1,0:T(8,128)S(1)} %get-tuple-element.19.own_ref, f32[16,2048]{1,0:T(8,128)S(1)} %get-tuple-element.20.ghost_ref), custom_call_target="tpu_custom_call" | custom-call | tf_op jit(solution)/shard_map/finish/pallas_call | solution.py:542

commit v5 on v4

--- a/solution.py
+++ b/solution.py
@@ -401,7 +401,8 @@
     )(conn, con)
 
 
-def combine_kernel(acc0, acc1, acc2, acc3, acc4, acc5, own_out, ghost_out, acc, pairs, summed, zin, ghost_sum, ghost_in,
+def combine_kernel(acc0, acc1, acc2, acc3, acc4, acc5, faces_hbm, own_out, acc, pairs, summed, zin, ghost_sum,
+                   ghost_in, faces_v, low_hot, stack, face_add, face_s,
                    p_ss, p_rs, z_ss, z_rs, g_ss, g_rs):
     m = lax.axis_index("mesh")
     h = lax.axis_index("harm")
@@ -412,6 +413,9 @@
     barrier = pltpu.get_barrier_semaphore()
     for peer in ((m, side), (m, far), (up, h), (down, h)):
         pl.semaphore_signal(barrier, inc=1, device_id=peer, device_id_type=MESH)
+
+    load = pltpu.make_async_copy(faces_hbm, faces_v, face_s)
+    load.start()
 
     bounds = [(OWN, FACE), (OWN + FACE, FACE)] + [(c * CHUNK, CHUNK) for c in range(PARTS)]
     chunks = [pl.ds(a, n) for a, n in bounds]
@@ -468,6 +472,15 @@
         summed[:, chunks[c]] = acc[block(far), chunks[c]] + pairs[1, :, chunks[c]]
         zs[c].start()
 
+    load.wait()
+    for f in range(2):
+        @pl.loop(0, FACE // 128)
+        def _(b):
+            column = faces_v[pl.ds(f, 1), pl.ds(pl.multiple_of(b * 128, 128), 128)] & 127
+            hot = jnp.where(lax.broadcasted_iota(jnp.int32, (128, 128), 0) == jnp.broadcast_to(column, (128, 128)),
+                            1.0, 0.0)
+            low_hot[pl.ds(pl.multiple_of(f * FACE + b * 128, 128), 128), :] = hot.T.astype(jnp.bfloat16)
+
     def total(c):
         own_pairs[c].wait_recv()
         zs[c].wait_recv()
@@ -476,79 +489,52 @@
     for f in range(2):
         ghost_sum[:, pl.ds(f * FACE, FACE)] = total(f)
         gs[f].start()
-    for c in range(2, count):
-        own_out[:, chunks[c]] = total(c)
     for g in gs:
         g.wait_recv()
-    ghost_out[...] = ghost_in[...]
+
+    @pl.loop(0, OWN // 1024)
+    def _(g):
+        for f in range(2):
+            part = pl.ds(f * FACE, FACE)
+            tile = jnp.broadcast_to(lax.shift_right_logical(faces_v[pl.ds(f, 1), :], 7), (16, FACE))
+            x = ghost_in[:, part]
+            high = x.astype(jnp.bfloat16).astype(jnp.float32)
+            rest = x - high
+            for u in range(8):
+                here = tile == g * 8 + u
+                stack[u * 32:u * 32 + 16, part] = jnp.where(here, high, 0.0).astype(jnp.bfloat16)
+                stack[u * 32 + 16:u * 32 + 32, part] = jnp.where(here, rest, 0.0).astype(jnp.bfloat16)
+        y = jnp.dot(stack[...], low_hot[...], preferred_element_type=jnp.float32)
+        for u in range(8):
+            face_add[:, pl.ds(pl.multiple_of((g * 8 + u) * 128, 128), 128)] = (
+                y[u * 32:u * 32 + 16, :] + y[u * 32 + 16:u * 32 + 32, :])
+
+    for c in range(2, count):
+        own_out[:, chunks[c]] = total(c) + face_add[:, chunks[c]]
     for c in (*far_pairs, *own_pairs, *zs, *gs):
         c.wait_send()
 
 
-def combine(accs):
+def combine(accs, faces):
     vmem = pl.BlockSpec(memory_space=pltpu.VMEM)
     dma = pltpu.SemaphoreType.DMA
     f32 = jnp.float32
     return pl.pallas_call(
         combine_kernel,
         name="combine",
-        out_shape=(jax.ShapeDtypeStruct((16, OWN), f32), jax.ShapeDtypeStruct((16, 2 * FACE), f32)),
-        in_specs=[vmem] * 6,
-        out_specs=(vmem, vmem),
+        out_shape=jax.ShapeDtypeStruct((16, OWN), f32),
+        in_specs=[vmem] * 6 + [pl.BlockSpec(memory_space=pltpu.HBM)],
+        out_specs=vmem,
         scratch_shapes=[
             pltpu.VMEM((64, EXT), f32), pltpu.VMEM((2, 16, EXT), f32), pltpu.VMEM((16, EXT), f32),
             pltpu.VMEM((16, EXT), f32), pltpu.VMEM((16, 2 * FACE), f32), pltpu.VMEM((16, 2 * FACE), f32),
+            pltpu.VMEM((2, FACE), jnp.int32), pltpu.VMEM((2 * FACE, 128), jnp.bfloat16),
+            pltpu.VMEM((256, 2 * FACE), jnp.bfloat16), pltpu.VMEM((16, OWN), f32), dma,
             dma((PARTS + 2, 2)), dma((PARTS + 2, 2)), dma((PARTS + 2,)), dma((PARTS + 2,)), dma((2,)), dma((2,)),
         ],
         compiler_params=pltpu.CompilerParams(collective_id=1, has_side_effects=True,
                                              vmem_limit_bytes=28 << 20),
-    )(*accs)
-
-
-def finish_kernel(faces_hbm, own_ref, ghost_ref, out_ref, ghost_t, full_t, faces_ref, idx_s):
-    loads = [pltpu.make_async_copy(faces_hbm.at[f], faces_ref.at[pl.ds(f * FACE, FACE)], idx_s.at[f])
-             for f in range(2)]
-    for c in loads:
-        c.start()
-
-    @pl.loop(0, OWN // 128, unroll=8)
-    def _(b):
-        full_t[pl.ds(pl.multiple_of(b * 128, 128), 128), :] = jnp.zeros((128, 16), jnp.float32)
-
-    @pl.loop(0, 2 * FACE // 128, unroll=8)
-    def _(b):
-        at = pl.ds(pl.multiple_of(b * 128, 128), 128)
-        ghost_t[at, :] = ghost_ref[:, at].T
-
-    for c in loads:
-        c.wait()
-
-    @pl.loop(0, 2 * FACE // 32)
-    def _(b):
-        rows = ghost_t.at[pl.ds(pl.multiple_of(b * 32, 32), 32), :]
-        for g in range(4):
-            near = faces_ref.at[pl.ds(pl.multiple_of(b * 32 + g * 8, 8), 8)]
-            for k in range(8):
-                full_t[pl.ds(near[k], 1), :] = rows[pl.ds(g * 8 + k, 1), :]
-
-    @pl.loop(0, OWN // 128, unroll=8)
-    def _(b):
-        at = pl.ds(pl.multiple_of(b * 128, 128), 128)
-        out_ref[:, at] = own_ref[:, at] + full_t[at, :].T
-
-
-def finish(faces, own, ghost):
-    vmem = pl.BlockSpec(memory_space=pltpu.VMEM)
-    return pl.pallas_call(
-        finish_kernel,
-        name="finish",
-        out_shape=jax.ShapeDtypeStruct((16, OWN), jnp.float32),
-        in_specs=[pl.BlockSpec(memory_space=pl.ANY), vmem, vmem],
-        out_specs=vmem,
-        scratch_shapes=[pltpu.VMEM((2 * FACE, 16), jnp.float32), pltpu.VMEM((OWN, 16), jnp.float32),
-                        pltpu.SMEM((2 * FACE,), jnp.int32), pltpu.SemaphoreType.DMA((2,))],
-        compiler_params=pltpu.CompilerParams(vmem_limit_bytes=40 << 20),
-    )(faces, own, ghost)
+    )(*accs, faces)
 
 
 def per_device(field_in, faces, connectivity, curl_vectors, operating_point, material, bh_knots, curve_base,
@@ -559,8 +545,7 @@
         for x in (field_in, point, material, curl_vectors, faces, connectivity, bh_knots, curve_base, curve_slopes)]
     contributions = forward(field_in, point, material, curl_vectors, faces, connectivity, bh_knots, curve_base,
                             curve_slopes)
-    own, ghost = combine(scatter(connectivity, contributions))
-    return finish(faces, own, ghost)
+    return combine(scatter(connectivity, contributions), faces)
 
 
 def solution(mesh):

time: 70.1 us -> 66.8 us (0.953)
  Pallas kernels: 69.7 us -> 65.7 us
  local copies, waits for them, and re-layouts: 0 us -> 0.73 us
    pallas_call x2 -> x1, Pallas kernels: 24.8 us -> 20.8 us  [combine(): pl.pallas_call(combine_kernel, name='combine', out_shape=jax.ShapeDtypeSt...]
    unnamed x0 -> x1, local copies, waits for them, and re-layouts: none -> 0.73 us
where the time goes in v5:
time: 66.8 us; the launch traced here: 66.5 us
  Pallas kernels  65.7 us (98%)
  local copies, waits for them, and re-layouts  0.73 us (1%)
    pallas_call x1, Pallas kernels, forward(): pl.pallas_call(forward_kernel, name='forward', out_shape=jax.ShapeDtypeSt...  36.4 us
    pallas_call x1, Pallas kernels, combine(): pl.pallas_call(combine_kernel, name='combine', out_shape=jax.ShapeDtypeSt...  20.8 us
    pallas_call x1, Pallas kernels, scatter(): pl.pallas_call(scatter_kernel, name='scatter', out_shape=(jax.ShapeDtypeS...  8.51 us

profile of v5, /device:TPU:1, one launch (start us, length us, event | category | flops | bytes accessed | tf_op | source)
XLA Modules:
  0.0 66.5 jit_solution(12160522756602726521)
XLA Ops:
  0.0 36.4 %forward.1.con_ref = f32[8,384,128]{2,1,0:T(8,128)S(1)} custom-call(f32[16,5120]{1,0:T(8,128)} %field_ref.1, f32[3,32,32,64]{3,2,1,0:T(8,128)} %bitcast.1, s32[32,32]{1,0:T(8,128)} %mat_ref.1, f32[3,6,4096]{2,1,0:T(8,128)} %curl_ref.1, s32[2,1024]{1,0:T(2,128)} %faces_hbm.3, s32[6,4096]{1,0:T(8,128)} %conn_hbm.3, s32[8]{0:T(128)} %knots_ref.1, f32[4]{0:T(128)} %base_ref.1, ...), custom_call_target="tpu_custom_call" | custom-call | tf_op jit(solution)/shard_map/forward/pallas_call | solution.py:332
  36.4 8.5 %scatter.1 = (f32[7168,128]{1,0:T(8,128)S(1)}, f32[7168,128]{1,0:T(8,128)S(1)}, f32[7168,128]{1,0:T(8,128)S(1)}, f32[7168,128]{1,0:T(8,128)S(1)}, f32[7168,128]{1,0:T(8,128)S(1)}, /*index=5*/f32[7168,128]{1,0:T(8,128)S(1)}) custom-call(s32[6,4096]{1,0:T(8,128)} %conn_hbm.3, f32[8,384,128]{2,1,0:T(8,128)S(1)} %forward.1.con_ref), custom_call_target="tpu_custom_call" | custom-call | tf_op jit(solution)/shard_map/scatter/pallas_call | solution.py:393
  44.9 20.8 %combine.1 = f32[16,5120]{1,0:T(8,128)S(1)} custom-call(f32[7168,128]{1,0:T(8,128)S(1)} %get-tuple-element.11.acc0, f32[7168,128]{1,0:T(8,128)S(1)} %get-tuple-element.12.acc1, f32[7168,128]{1,0:T(8,128)S(1)} %get-tuple-element.13.acc2, f32[7168,128]{1,0:T(8,128)S(1)} %get-tuple-element.14.acc3, f32[7168,128]{1,0:T(8,128)S(1)} %get-tuple-element.15.acc4, ...), custom_call_target="tpu_custom_call" | custom-call | tf_op jit(solution)/shard_map/combine/pallas_call | solution.py:522
  65.7 0.7 %copy.13 = f32[16,5120]{1,0:T(8,128)} copy(f32[16,5120]{1,0:T(8,128)S(1)} %combine.1) | data formatting | bytes 655360

commit v6 on v5

--- a/solution.py
+++ b/solution.py
@@ -54,7 +54,8 @@
 def forward_kernel(field_ref, point_ref, mat_ref, curl_ref, faces_hbm, conn_hbm, knots_ref, base_ref, slopes_ref,
                    inv_hbm, fwd_hbm, out_ref,
                    field, point, curl, opsend, op_in, field_t, face_rows, face_cols, ext, ext2, curl_t, wide, got, flux, inv_ref, fwd_ref, faces_ref, conn_ref,
-                   in_s, op_ss, op_rs, far_ss, far_rs, side_ss, side_rs, gh_ss, gh_rs, fw_ss, fw_rs, rel_ss, rel_rs, idx_s):
+                   in_s, op_ss, op_rs, far_ss, far_rs, side_ss, side_rs, gh_ss, gh_rs, fw_ss, fw_rs, rel_ss, rel_rs, idx_s,
+                   go_near, go_all):
     m = lax.axis_index("mesh")
     h = lax.axis_index("harm")
     up, down = lax.rem(m + 1, N_MESH), lax.rem(m + N_MESH - 1, N_MESH)
@@ -68,19 +69,27 @@
 
     within = lax.rem(m, 16)
     barrier = pltpu.get_barrier_semaphore()
-    crossing_h = [h, far]
-    for peer in ((m, far), (m, side), (up, h), (down, h)):
-        pl.semaphore_signal(barrier, inc=1, device_id=peer, device_id_type=MESH)
+    core = lax.rem(h, 2)
+    leader, desk = h - core, h - core + 1
+    far_leader, far_desk = lax.rem(leader + 2, 4), lax.rem(desk + 2, 4)
+    pl.semaphore_signal(barrier, inc=1, device_id=(m, far_leader), device_id_type=MESH)
+
+    @pl.when(core == 1)
+    def _():
+        pl.semaphore_signal(barrier, inc=1, device_id=(m, leader), device_id_type=MESH)
+
+    for peer in (up, down):
+        pl.semaphore_signal(barrier, inc=1, device_id=(peer, desk), device_id_type=MESH)
 
     @pl.loop(1, 16, unroll=3)
     def _(d):
         other = lax.rem(within + d, 16)
-        pl.semaphore_signal(barrier, inc=1, device_id=(half * 16 + other, h), device_id_type=MESH)
+        pl.semaphore_signal(barrier, inc=1, device_id=(half * 16 + other, desk), device_id_type=MESH)
 
     for odd in range(2):
         @pl.loop(0, 8, unroll=2)
         def _(d):
-            pl.semaphore_signal(barrier, inc=1, device_id=((1 - half) * 16 + 2 * d + odd, crossing_h[odd]),
+            pl.semaphore_signal(barrier, inc=1, device_id=((1 - half) * 16 + 2 * d + odd, (desk, far_desk)[odd]),
                                 device_id_type=MESH)
 
     load_field = pltpu.make_async_copy(field_ref, field, in_s.at[0])
@@ -100,7 +109,14 @@
 
     load_field.wait()
 
-    pl.semaphore_wait(barrier, N_MESH - 1 + 4)
+    @pl.when(core == 0)
+    def _():
+        pl.semaphore_wait(barrier, 3)
+        pl.semaphore_signal(go_near, inc=1, device_id=(m, side), device_id_type=MESH)
+
+    @pl.when(core == 1)
+    def _():
+        pl.semaphore_wait(go_near, 1)
 
     def rows_of(who):
         return pl.ds(pl.multiple_of(16 * who, 16), 16)
@@ -149,6 +165,15 @@
             dst_ref=ext.at[rows_of(h), pl.ds(OWN + (1 - f) * FACE, FACE)],
             send_sem=gh_ss.at[f], recv_sem=gh_rs.at[f],
             device_id=(peer, h), device_id_type=MESH)
+
+    @pl.when(core == 1)
+    def _():
+        pl.semaphore_wait(barrier, 2 * (N_MESH - 1 + 2))
+        pl.semaphore_signal(go_all, inc=1, device_id=(m, side), device_id_type=MESH)
+
+    @pl.when(core == 0)
+    def _():
+        pl.semaphore_wait(go_all, 1)
 
     ghosts = [ghost_copy(0, down), ghost_copy(1, up)]
     for c in ghosts:
@@ -345,6 +370,7 @@
             pltpu.SMEM((2 * FACE,), jnp.int32), pltpu.SMEM((6 * 4096,), jnp.int32),
             dma((5,)), dma, dma, dma((PARTS,)), dma((PARTS,)), dma((PARTS,)), dma((PARTS,)),
             dma((2,)), dma((2,)), dma((2,)), dma((2,)), dma((PARTS + 1,)), dma((PARTS + 1,)), dma((10,)),
+            pltpu.SemaphoreType.REGULAR, pltpu.SemaphoreType.REGULAR,
         ],
         compiler_params=pltpu.CompilerParams(collective_id=0, has_side_effects=True,
                                              vmem_limit_bytes=34 << 20),

time: 66.8 us -> 64.3 us (0.963)
  Pallas kernels: 65.7 us -> 63.2 us
    pallas_call x1, Pallas kernels: 20.8 us -> 18.3 us  [combine(): pl.pallas_call(combine_kernel, name='combine', out_shape=jax.ShapeDtypeSt...]
where the time goes in v6:
time: 64.3 us; the launch traced here: 64 us
  Pallas kernels  63.2 us (98%)
  local copies, waits for them, and re-layouts  0.73 us (1%)
    pallas_call x1, Pallas kernels, forward(): pl.pallas_call(forward_kernel, name='forward', out_shape=jax.ShapeDtypeSt...  36.4 us
    pallas_call x1, Pallas kernels, combine(): pl.pallas_call(combine_kernel, name='combine', out_shape=jax.ShapeDtypeSt...  18.3 us
    pallas_call x1, Pallas kernels, scatter(): pl.pallas_call(scatter_kernel, name='scatter', out_shape=(jax.ShapeDtypeS...  8.51 us

profile of v6, /device:TPU:1, one launch (start us, length us, event | category | flops | bytes accessed | tf_op | source)
XLA Modules:
  0.0 64.0 jit_solution(170672381452949772)
XLA Ops:
  0.0 36.4 %forward.1.con_ref = f32[8,384,128]{2,1,0:T(8,128)S(1)} custom-call(f32[16,5120]{1,0:T(8,128)} %field_ref.1, f32[3,32,32,64]{3,2,1,0:T(8,128)} %bitcast.1, s32[32,32]{1,0:T(8,128)} %mat_ref.1, f32[3,6,4096]{2,1,0:T(8,128)} %curl_ref.1, s32[2,1024]{1,0:T(2,128)} %faces_hbm.3, s32[6,4096]{1,0:T(8,128)} %conn_hbm.3, s32[8]{0:T(128)} %knots_ref.1, f32[4]{0:T(128)} %base_ref.1, ...), custom_call_target="tpu_custom_call" | custom-call | tf_op jit(solution)/shard_map/forward/pallas_call | solution.py:357
  36.4 8.5 %scatter.1 = (f32[7168,128]{1,0:T(8,128)S(1)}, f32[7168,128]{1,0:T(8,128)S(1)}, f32[7168,128]{1,0:T(8,128)S(1)}, f32[7168,128]{1,0:T(8,128)S(1)}, f32[7168,128]{1,0:T(8,128)S(1)}, /*index=5*/f32[7168,128]{1,0:T(8,128)S(1)}) custom-call(s32[6,4096]{1,0:T(8,128)} %conn_hbm.3, f32[8,384,128]{2,1,0:T(8,128)S(1)} %forward.1.con_ref), custom_call_target="tpu_custom_call" | custom-call | tf_op jit(solution)/shard_map/scatter/pallas_call | solution.py:419
  44.9 18.3 %combine.1 = f32[16,5120]{1,0:T(8,128)S(1)} custom-call(f32[7168,128]{1,0:T(8,128)S(1)} %get-tuple-element.11.acc0, f32[7168,128]{1,0:T(8,128)S(1)} %get-tuple-element.12.acc1, f32[7168,128]{1,0:T(8,128)S(1)} %get-tuple-element.13.acc2, f32[7168,128]{1,0:T(8,128)S(1)} %get-tuple-element.14.acc3, f32[7168,128]{1,0:T(8,128)S(1)} %get-tuple-element.15.acc4, ...), custom_call_target="tpu_custom_call" | custom-call | tf_op jit(solution)/shard_map/combine/pallas_call | solution.py:548
  63.3 0.7 %copy.13 = f32[16,5120]{1,0:T(8,128)} copy(f32[16,5120]{1,0:T(8,128)S(1)} %combine.1) | data formatting | bytes 655360

commit v7 on v6

--- a/solution.py
+++ b/solution.py
@@ -198,24 +198,26 @@
             send_sem=op_ss, recv_sem=op_rs,
             device_id=(p, target), device_id_type=MESH)
 
+    op_keep = pltpu.make_async_copy(opsend.at[m], op_in.at[m], in_s.at[4])
+    op_keep.start()
+
+    for c in ghosts:
+        c.wait_recv()
+
+    def gfwd_copy(n, peer):
+        return pltpu.make_async_remote_copy(
+            src_ref=ext.at[rows_of(h), ghost_cols], dst_ref=ext.at[rows_of(h), ghost_cols],
+            send_sem=fw_ss.at[n], recv_sem=fw_rs.at[n],
+            device_id=(m, peer), device_id_type=MESH)
+
+    gfar, gside = gfwd_copy(0, far), gfwd_copy(1, side)
+    gfar.start()
+    gside.start()
+
     @pl.loop(1, 16)
     def _(slot):
         op_copy(slot).start()
-    op_keep = pltpu.make_async_copy(opsend.at[m], op_in.at[m], in_s.at[4])
-    op_keep.start()
-
-    for c in ghosts:
-        c.wait_recv()
-
-    def gfwd_copy(n, peer):
-        return pltpu.make_async_remote_copy(
-            src_ref=ext.at[rows_of(h), ghost_cols], dst_ref=ext.at[rows_of(h), ghost_cols],
-            send_sem=fw_ss.at[n], recv_sem=fw_rs.at[n],
-            device_id=(m, peer), device_id_type=MESH)
-
-    gfar, gside = gfwd_copy(0, far), gfwd_copy(1, side)
-    gfar.start()
-    gside.start()
+
 
     def relay(c, cols):
         return pltpu.make_async_remote_copy(

time: 64.3 us -> 64.1 us (level)
  no operation moved by 1% of the time
where the time goes in v7:
time: 64.1 us; the launch traced here: 63.8 us
  Pallas kernels  63 us (98%)
  local copies, waits for them, and re-layouts  0.73 us (1%)
    pallas_call x1, Pallas kernels, forward(): pl.pallas_call(forward_kernel, name='forward', out_shape=jax.ShapeDtypeSt...  36.2 us
    pallas_call x1, Pallas kernels, combine(): pl.pallas_call(combine_kernel, name='combine', out_shape=jax.ShapeDtypeSt...  18.3 us
    pallas_call x1, Pallas kernels, scatter(): pl.pallas_call(scatter_kernel, name='scatter', out_shape=(jax.ShapeDtypeS...  8.51 us

profile of v7, /device:TPU:1, one launch (start us, length us, event | category | flops | bytes accessed | tf_op | source)
XLA Modules:
  0.0 63.8 jit_solution(11746048384969648078)
XLA Ops:
  0.0 36.2 %forward.1.con_ref = f32[8,384,128]{2,1,0:T(8,128)S(1)} custom-call(f32[16,5120]{1,0:T(8,128)} %field_ref.1, f32[3,32,32,64]{3,2,1,0:T(8,128)} %bitcast.1, s32[32,32]{1,0:T(8,128)} %mat_ref.1, f32[3,6,4096]{2,1,0:T(8,128)} %curl_ref.1, s32[2,1024]{1,0:T(2,128)} %faces_hbm.3, s32[6,4096]{1,0:T(8,128)} %conn_hbm.3, s32[8]{0:T(128)} %knots_ref.1, f32[4]{0:T(128)} %base_ref.1, ...), custom_call_target="tpu_custom_call" | custom-call | tf_op jit(solution)/shard_map/forward/pallas_call | solution.py:359
  36.2 8.5 %scatter.1 = (f32[7168,128]{1,0:T(8,128)S(1)}, f32[7168,128]{1,0:T(8,128)S(1)}, f32[7168,128]{1,0:T(8,128)S(1)}, f32[7168,128]{1,0:T(8,128)S(1)}, f32[7168,128]{1,0:T(8,128)S(1)}, /*index=5*/f32[7168,128]{1,0:T(8,128)S(1)}) custom-call(s32[6,4096]{1,0:T(8,128)} %conn_hbm.3, f32[8,384,128]{2,1,0:T(8,128)S(1)} %forward.1.con_ref), custom_call_target="tpu_custom_call" | custom-call | tf_op jit(solution)/shard_map/scatter/pallas_call | solution.py:421
  44.7 18.3 %combine.1 = f32[16,5120]{1,0:T(8,128)S(1)} custom-call(f32[7168,128]{1,0:T(8,128)S(1)} %get-tuple-element.11.acc0, f32[7168,128]{1,0:T(8,128)S(1)} %get-tuple-element.12.acc1, f32[7168,128]{1,0:T(8,128)S(1)} %get-tuple-element.13.acc2, f32[7168,128]{1,0:T(8,128)S(1)} %get-tuple-element.14.acc3, f32[7168,128]{1,0:T(8,128)S(1)} %get-tuple-element.15.acc4, ...), custom_call_target="tpu_custom_call" | custom-call | tf_op jit(solution)/shard_map/combine/pallas_call | solution.py:550
  63.0 0.7 %copy.13 = f32[16,5120]{1,0:T(8,128)} copy(f32[16,5120]{1,0:T(8,128)S(1)} %combine.1) | data formatting | bytes 655360

commit v8 on v7

--- a/solution.py
+++ b/solution.py
@@ -393,11 +393,11 @@
     for c in loads:
         c.start()
 
-    @pl.loop(0, EXT // 64)
+    @pl.loop(0, EXT // 256)
     def _(b):
-        at = pl.ds(pl.multiple_of(b * 64, 64), 64)
+        at = pl.ds(pl.multiple_of(b * 256, 256), 256)
         for a in accs:
-            a[at, :] = jnp.zeros((64, 128), jnp.float32)
+            a[at, :] = jnp.zeros((256, 128), jnp.float32)
 
     for c in loads:
         c.wait()

time: 64.1 us -> 64.1 us (level)
  no operation moved by 1% of the time
where the time goes in v8:
time: 64.1 us; the launch traced here: 63.7 us
  Pallas kernels  63 us (98%)
  local copies, waits for them, and re-layouts  0.73 us (1%)
    pallas_call x1, Pallas kernels, forward(): pl.pallas_call(forward_kernel, name='forward', out_shape=jax.ShapeDtypeSt...  36.2 us
    pallas_call x1, Pallas kernels, combine(): pl.pallas_call(combine_kernel, name='combine', out_shape=jax.ShapeDtypeSt...  18.3 us
    pallas_call x1, Pallas kernels, scatter(): pl.pallas_call(scatter_kernel, name='scatter', out_shape=(jax.ShapeDtypeS...  8.51 us

profile of v8, /device:TPU:1, one launch (start us, length us, event | category | flops | bytes accessed | tf_op | source)
XLA Modules:
  0.0 63.7 jit_solution(13788125802790867018)
XLA Ops:
  0.0 36.2 %forward.1.con_ref = f32[8,384,128]{2,1,0:T(8,128)S(1)} custom-call(f32[16,5120]{1,0:T(8,128)} %field_ref.1, f32[3,32,32,64]{3,2,1,0:T(8,128)} %bitcast.1, s32[32,32]{1,0:T(8,128)} %mat_ref.1, f32[3,6,4096]{2,1,0:T(8,128)} %curl_ref.1, s32[2,1024]{1,0:T(2,128)} %faces_hbm.3, s32[6,4096]{1,0:T(8,128)} %conn_hbm.3, s32[8]{0:T(128)} %knots_ref.1, f32[4]{0:T(128)} %base_ref.1, ...), custom_call_target="tpu_custom_call" | custom-call | tf_op jit(solution)/shard_map/forward/pallas_call | solution.py:359
  36.2 8.5 %scatter.1 = (f32[7168,128]{1,0:T(8,128)S(1)}, f32[7168,128]{1,0:T(8,128)S(1)}, f32[7168,128]{1,0:T(8,128)S(1)}, f32[7168,128]{1,0:T(8,128)S(1)}, f32[7168,128]{1,0:T(8,128)S(1)}, /*index=5*/f32[7168,128]{1,0:T(8,128)S(1)}) custom-call(s32[6,4096]{1,0:T(8,128)} %conn_hbm.3, f32[8,384,128]{2,1,0:T(8,128)S(1)} %forward.1.con_ref), custom_call_target="tpu_custom_call" | custom-call | tf_op jit(solution)/shard_map/scatter/pallas_call | solution.py:421
  44.7 18.3 %combine.1 = f32[16,5120]{1,0:T(8,128)S(1)} custom-call(f32[7168,128]{1,0:T(8,128)S(1)} %get-tuple-element.11.acc0, f32[7168,128]{1,0:T(8,128)S(1)} %get-tuple-element.12.acc1, f32[7168,128]{1,0:T(8,128)S(1)} %get-tuple-element.13.acc2, f32[7168,128]{1,0:T(8,128)S(1)} %get-tuple-element.14.acc3, f32[7168,128]{1,0:T(8,128)S(1)} %get-tuple-element.15.acc4, ...), custom_call_target="tpu_custom_call" | custom-call | tf_op jit(solution)/shard_map/combine/pallas_call | solution.py:550
  63.0 0.7 %copy.13 = f32[16,5120]{1,0:T(8,128)} copy(f32[16,5120]{1,0:T(8,128)S(1)} %combine.1) | data formatting | bytes 655360
